TPU v7x, 256 devices: a whole 4x4x8 slice. The times are simulated.
256 devices in a mesh: req: 16 (over z_hi, x), mp: 16 (over z_lo, y, core).
Axes of the slice: x: 4, y: 4, z: 8 (z_hi: 4, z_lo: 2; z = z_hi * 2 + z_lo), core: 2. Of those that a mesh axis runs over, the one named last changes fastest.
Arguments:
- queries: bfloat16 [2048, 4096], P('req', 'mp'), may hold values from -6 to 6
- suffix_kv: bfloat16 [2, 2048, 4096], P(None, 'req', 'mp'), may hold values from -6 to 6
- prefix_kv: bfloat16 [2, 8192, 4096], P(None, 'req', 'mp'), may hold values from -6 to 6
- resid: bfloat16 [2048, 4096], P('req', 'mp'), may hold values from -6 to 6
- ln_gain: float32 [4096], replicated, may hold values from 0.1 to 1.9
- out_weight: bfloat16 [4096, 4096], P('mp'), may hold values from -0.125 to 0.125
- up_weight: bfloat16 [4096, 8192], P(None, 'mp'), may hold values from -0.09375 to 0.09375
- down_weight: bfloat16 [8192, 4096], P('mp'), may hold values from -0.09375 to 0.09375
- lengths: int32 [16], replicated, may hold values from 1 to 128, 1024 in all
- req_group: int32 [16], replicated, may hold values from 0 to 3, as said below
- prefix_owner: int32 [16], replicated, may hold values from 0 to 15, as said below
Outputs:
- attended: bfloat16 [2048, 4096], P('req', 'mp')
- layer_out: bfloat16 [2048, 4096], P('req', 'mp')
Inputs may be any that keep to these rules, and one draw needn't show every extreme that they name: `req_group`: each of the 4 groups holds exactly 4 requests. `prefix_owner`: a permutation: every logical block is held by exactly one stored block.
All inputs are finite; a program needn't handle non-finite values.
Results may differ from a plain program's by a relative error of at most 0.029.
Values may be sent and summed in bfloat16 or wider, within the bound.
A program may use at most 128 MiB of HBM per device.

v0:
```python
import jax
import jax.numpy as jnp
from jax import lax
from jax.sharding import PartitionSpec as P

H = 32
DH = 128
KB = 512
S_MAX = 128
P_SIZE = 2048


very_negative = -1e30


def block_partial(query_rows, key_rows, value_rows, query_pos, key_pos, allowed, slopes, shared):
    if shared:
        score_form = "rqhd,khd->rqhk"
        value_form = "rqhk,khd->rqhd"
    else:
        score_form = "rqhd,rkhd->rqhk"
        value_form = "rqhk,rkhd->rqhd"
    scores = jnp.einsum(
        score_form, query_rows, key_rows, preferred_element_type=jnp.float32
    ) * float(DH) ** (-0.5)
    distance = (query_pos[:, None, None] - key_pos[None, None, :]).astype(jnp.float32)
    scores = scores - slopes[None, :, None] * distance
    masked = jnp.where(allowed, scores, very_negative)
    maxima = jnp.max(masked, axis=-1)
    weights = jnp.where(allowed, jnp.exp(masked - maxima[..., None]), 0.0)
    totals = jnp.sum(weights, axis=-1)
    rounded = weights.astype(jnp.bfloat16)
    weighted = jnp.einsum(value_form, rounded, value_rows, preferred_element_type=jnp.float32)
    return (weighted, maxima, totals)


def combine(first_part, second_part):
    peak_max = jnp.maximum(first_part[1], second_part[1])
    scale_first = jnp.exp(first_part[1] - peak_max)
    scale_second = jnp.exp(second_part[1] - peak_max)
    weighted = first_part[0] * scale_first[..., None] + second_part[0] * scale_second[..., None]
    return (weighted, peak_max, first_part[2] * scale_first + second_part[2] * scale_second)


def shards(
    queries,
    suffix_kv,
    prefix_kv,
    resid,
    ln_gain,
    out_weight,
    up_weight,
    down_weight,
    lengths,
    req_group,
    prefix_owner,
):
    row_count = queries.shape[0]
    local_req = row_count // S_MAX
    columns = queries.shape[1]
    head_count = columns // DH
    per_group = P_SIZE // KB
    first_req = lax.axis_index("req") * local_req
    col_start = lax.axis_index("mp") * columns
    my_len = lax.dynamic_slice_in_dim(lengths, first_req, local_req)
    my_group = lax.dynamic_slice_in_dim(req_group, first_req, local_req)
    head_ids = (lax.axis_index("mp") * head_count + jnp.arange(head_count)).astype(jnp.float32)
    slopes = jnp.power(2.0, -8.0 * (head_ids + 1.0) / H)
    my_query = queries.reshape(local_req, S_MAX, head_count, DH)
    suffix_local = suffix_kv.reshape(2, local_req, S_MAX, head_count, DH)
    offsets = jnp.arange(S_MAX)
    query_pos = P_SIZE + offsets
    allowed = (offsets[None, None, :] <= offsets[None, :, None]) & (
        offsets[None, None, :] < my_len[:, None, None]
    )
    own_part = block_partial(
        my_query,
        suffix_local[0],
        suffix_local[1],
        query_pos,
        query_pos,
        allowed[:, :, None, :],
        slopes,
        False,
    )
    key_offsets = jnp.arange(KB)
    shard_piece = lax.all_gather(prefix_kv, "req", axis=1, tiled=True)
    block_total = shard_piece.shape[1] // KB
    blocks_here = shard_piece.reshape(2, block_total, KB, head_count, DH)

    def fold_step(block_index, inner_state):
        logical = prefix_owner[block_index]
        same_group = my_group == logical // per_group
        base_pos = logical % per_group * KB

        def attend_block(state_in):
            fresh = block_partial(
                my_query,
                blocks_here[0, block_index],
                blocks_here[1, block_index],
                query_pos,
                base_pos + key_offsets,
                same_group[:, None, None, None],
                slopes,
                True,
            )
            return combine(state_in, fresh)

        return lax.cond(jnp.any(same_group), attend_block, lambda state_in: state_in, inner_state)

    result = lax.fori_loop(0, block_total, fold_step, own_part)
    outcome = result[0] / result[2][..., None]
    live_mask = offsets[None, :] < my_len[:, None]
    attended = (
        jnp.where(live_mask[:, :, None, None], outcome, 0.0)
        .astype(jnp.bfloat16)
        .reshape(row_count, columns)
    )
    head_term = jnp.dot(attended, out_weight, preferred_element_type=jnp.float32)
    own_columns = lax.dynamic_slice_in_dim(head_term, col_start, columns, 1) + resid.astype(
        jnp.float32
    )
    head_term = lax.dynamic_update_slice_in_dim(head_term, own_columns, col_start, 1)
    mixed_rows = lax.psum(head_term.astype(jnp.bfloat16), "mp").astype(jnp.float32)
    row_mean = jnp.mean(mixed_rows, axis=1, keepdims=True)
    centered = mixed_rows - row_mean
    variance = jnp.mean(centered * centered, axis=1, keepdims=True)
    normed = (centered * lax.rsqrt(variance + 1e-05) * ln_gain).astype(jnp.bfloat16)
    hidden = jax.nn.gelu(
        jnp.dot(normed, up_weight, preferred_element_type=jnp.float32), approximate=False
    ).astype(jnp.bfloat16)
    projected = jnp.dot(hidden, down_weight, preferred_element_type=jnp.float32)
    update = lax.psum_scatter(
        projected.astype(jnp.bfloat16), "mp", scatter_dimension=1, tiled=True
    ).astype(jnp.float32)
    mixed_own = lax.dynamic_slice_in_dim(mixed_rows, col_start, columns, 1)
    layer_out = jnp.where(live_mask.reshape(row_count)[:, None], mixed_own + update, 0.0).astype(
        jnp.bfloat16
    )
    return (attended, layer_out)


def solution(mesh):
    placed = (
        P("req", "mp"),
        P(None, "req", "mp"),
        P(None, "req", "mp"),
        P("req", "mp"),
        P(),
        P("mp", None),
        P(None, "mp"),
        P("mp", None),
        P(),
        P(),
        P(),
    )
    return jax.shard_map(
        shards,
        mesh=mesh,
        in_specs=placed,
        out_specs=(P("req", "mp"), P("req", "mp")),
        check_vma=False,
    )
```

profile of v0, /device:TPU:1, one launch (start us, length us, event | category | flops | bytes accessed | tf_op | source)
XLA Modules:
  0.0 438.3 jit_solution(7493433449119299911)
XLA Ops:
  7.2 0.7 all-gather.2.cloned.1.call-update
  8.0 1.2 dynamic_slice.35
  9.2 1.2 dynamic_slice.34
  10.4 0.9 copy.28
  11.5 0.9 fusion.121
  12.6 0.6 iota_compare_fusion.1
  13.4 1.1 fusion.122
  14.9 102.8 %all-gather.2.cloned.1.call-done = bf16[2,8192,256]{2,1,0:T(8,128)(2,1)} async-done(((bf16[2,512,256]{2,1,0:T(8,128)(2,1)}), bf16[2,8192,256]{2,1,0:T(8,128)(2,1)}) %all-gather.2.cloned.1.call-update) | async-done | bytes 8388624 | tf_op jit(solution)/shard_map/all_gather | solution.py:87
  117.7 12.5 %reshape.277 = bf16[2,16,512,2,128]{4,3,2,1,0:T(2,128)(2,1)} reshape(bf16[2,8192,256]{2,1,0:T(8,128)(2,1)} %all-gather.2.cloned.1.call-done) | data formatting | bytes 16777216 | tf_op jit(solution)/shard_map/reshape | solution.py:89
  130.3 8.8 %copy.30 = bf16[2,16,512,2,128]{4,2,3,1,0:T(8,128)(2,1)} copy(bf16[2,16,512,2,128]{4,3,2,1,0:T(2,128)(2,1)} %reshape.277) | data formatting | bytes 16777216
  139.1 79.0 %while.20 = (s32[]{:T(128)}, f32[1,128,2,128]{1,3,2,0:T(8,128)S(1)}, f32[1,128,2]{1,2,0:T(2,128)S(1)}, f32[1,128,2]{1,2,0:T(2,128)S(1)}, s32[16]{0:T(128)S(1)}, ...) while((s32[]{:T(128)}, ...), condition=%wide.region_7.8_spmd.clone, body=%wide.region_2.7_spmd.clone.sunk | while | flops 68782248 | bytes 2980505 | solution.py:111
  139.1 0.6 dynamic_slice.54
  142.8 0.6 dynamic_slice.54
  146.6 0.6 dynamic_slice.54
  150.3 4.7 %conditional.3 = ((f32[1,128,2,128]{1,3,2,0:T(8,128)S(1)}, f32[1,128,2]{1,2,0:T(2,128)S(1)}, f32[1,128,2]{1,2,0:T(2,128)S(1)})) conditional(s32[]{:T(128)} %bitcast.111, (f32[1,128,2,128]{1,3,2,0:T(8,128)S(1)}, f32[1,128,2]{1,2,0:T(2,128)S(1)}, f32[1,128,2]{1,2,0:T(2,128)S(1)}) %tuple.96, (pred[1]{0:T(512)(128)(4,1)}, s32[]{:T(128)}, ...), branch_computations={%region_3.3_spmd, %region_4.6_spmd.clone} | conditional | flops 68782224 | bytes 2977504 | solution.py:109
  152.4 1.2 fusion.120
  153.8 1.3 fusion.10
  155.0 0.6 dynamic_slice.54
  158.8 4.7 %conditional.3 = ((f32[1,128,2,128]{1,3,2,0:T(8,128)S(1)}, f32[1,128,2]{1,2,0:T(2,128)S(1)}, f32[1,128,2]{1,2,0:T(2,128)S(1)})) conditional(s32[]{:T(128)} %bitcast.111, (f32[1,128,2,128]{1,3,2,0:T(8,128)S(1)}, f32[1,128,2]{1,2,0:T(2,128)S(1)}, f32[1,128,2]{1,2,0:T(2,128)S(1)}) %tuple.96, (pred[1]{0:T(512)(128)(4,1)}, s32[]{:T(128)}, ...), branch_computations={%region_3.3_spmd, %region_4.6_spmd.clone} | conditional | flops 68782224 | bytes 2977504 | solution.py:109
  160.9 1.2 fusion.120
  162.2 1.3 fusion.10
  163.5 0.6 dynamic_slice.54
  167.3 0.6 dynamic_slice.54
  171.0 4.7 %conditional.3 = ((f32[1,128,2,128]{1,3,2,0:T(8,128)S(1)}, f32[1,128,2]{1,2,0:T(2,128)S(1)}, f32[1,128,2]{1,2,0:T(2,128)S(1)})) conditional(s32[]{:T(128)} %bitcast.111, (f32[1,128,2,128]{1,3,2,0:T(8,128)S(1)}, f32[1,128,2]{1,2,0:T(2,128)S(1)}, f32[1,128,2]{1,2,0:T(2,128)S(1)}) %tuple.96, (pred[1]{0:T(512)(128)(4,1)}, s32[]{:T(128)}, ...), branch_computations={%region_3.3_spmd, %region_4.6_spmd.clone} | conditional | flops 68782224 | bytes 2977504 | solution.py:109
  173.1 1.2 fusion.120
  174.4 1.3 fusion.10
  175.7 0.6 dynamic_slice.54
  179.5 0.6 dynamic_slice.54
  183.3 0.6 dynamic_slice.54
  187.0 0.6 dynamic_slice.54
  190.7 4.7 %conditional.3 = ((f32[1,128,2,128]{1,3,2,0:T(8,128)S(1)}, f32[1,128,2]{1,2,0:T(2,128)S(1)}, f32[1,128,2]{1,2,0:T(2,128)S(1)})) conditional(s32[]{:T(128)} %bitcast.111, (f32[1,128,2,128]{1,3,2,0:T(8,128)S(1)}, f32[1,128,2]{1,2,0:T(2,128)S(1)}, f32[1,128,2]{1,2,0:T(2,128)S(1)}) %tuple.96, (pred[1]{0:T(512)(128)(4,1)}, s32[]{:T(128)}, ...), branch_computations={%region_3.3_spmd, %region_4.6_spmd.clone} | conditional | flops 68782224 | bytes 2977504 | solution.py:109
  192.8 1.2 fusion.120
  194.2 1.3 fusion.10
  195.5 0.6 dynamic_slice.54
  199.2 0.6 dynamic_slice.54
  203.0 0.6 dynamic_slice.54
  206.8 0.6 dynamic_slice.54
  210.5 0.6 dynamic_slice.54
  214.3 0.6 dynamic_slice.54
  218.9 1.2 convert_element_type.80
  220.2 137.1 %all-reduce.2.cloned.1.call-done = bf16[128,4096]{1,0:T(8,128)(2,1)} async-done(((bf16[128,4096]{1,0:T(8,128)(2,1)}), bf16[128,4096]{1,0:T(8,128)(2,1)}) %all-reduce.2.cloned.1.call-update) | async-done | bytes 1048592 | tf_op jit(solution)/shard_map/psum | solution.py:124
  357.3 1.5 convert_reduce_fusion
  358.8 1.7 multiply_reduce_fusion
  360.5 6.4 %convolution_convert_fusion = bf16[128,4096]{1,0:T(8,128)(2,1)} fusion(bf16[512,4096]{1,0:T(8,128)(2,1)} %param.22, bf16[4096,512]{1,0:T(8,128)(2,1)} %param.21, bf16[128,4096]{1,0:T(8,128)(2,1)S(1)} %copy-done.1, f32[4096]{0:T(1024)S(1)} %copy-done.3, f32[128]{0:T(128)S(1)} %add_rsqrt_fusion, f32[128]{0:T(128)S(1)} %broadcast_multiply_fusion), kind=kOutput, calls=%fused_computation.40 | convolution fusion | flops 1081147392 | bytes 10503168 | tf_op jit(solution)/shard_map/dot_general | solution.py:132
  367.0 0.7 copy.32
  367.7 1.6 convert_element_type.81
  369.3 60.8 %reduce-scatter.2.cloned.1.call-done = bf16[128,256]{1,0:T(8,128)(2,1)} async-done(((bf16[128,4096]{1,0:T(8,128)(2,1)}), bf16[128,256]{1,0:T(8,128)(2,1)}) %reduce-scatter.2.cloned.1.call-update) | async-done | bytes 65552 | tf_op jit(solution)/shard_map/reduce_scatter | solution.py:133
  430.1 1.7 select_convert_fusion
  (122 shorter events, 3.5 us)
Async XLA Ops:
  7.2 210.9 %copy-start = (bf16[256,4096]{1,0:T(8,128)(2,1)S(1)}, bf16[256,4096]{1,0:T(8,128)(2,1)}, u32[]{:S(2)}) copy-start(bf16[256,4096]{1,0:T(8,128)(2,1)} %param.20) | copy-start | bytes 6291460
  7.2 110.5 %all-gather.2.cloned.1.call-start = ((), (), s32[]{:S(2)}) async-start(), calls=%async_computation.1 | async-start | bytes 8912896 | tf_op jit(solution)/shard_map/all_gather | solution.py:87
  7.9 349.4 %all-reduce.2.cloned.1.call-start = ((), (), s32[]{:S(2)}) async-start(), calls=%async_computation.2 | async-start | bytes 2097152 | tf_op jit(solution)/shard_map/psum | solution.py:124
  130.3 8.8 %copy-start.4 = (s32[16]{0:T(128)S(1)}, s32[16]{0:T(128)}, u32[]{:S(2)}) copy-start(s32[16]{0:T(128)} %param.25) | copy-start | bytes 196
  218.1 0.8 copy-start.2
  220.1 140.4 %copy-start.3 = (f32[4096]{0:T(1024)S(1)}, f32[4096]{0:T(1024)}, u32[]{:S(2)}) copy-start(f32[4096]{0:T(1024)} %param.19) | copy-start | bytes 49156
  220.1 209.9 %reduce-scatter.2.cloned.1.call-start = ((), (), s32[]{:S(2)}) async-start(), calls=%async_computation.3 | async-start | bytes 1114112 | tf_op jit(solution)/shard_map/reduce_scatter | solution.py:133
  357.3 3.2 copy-start.1
Sparse Core Ops, SparseCore 0:
  10.4 107.2 all-gather.1
  220.3 136.9 all-reduce.1
  367.1 62.9 reduce-scatter.1
where the time goes:
time: 442 us; the launch traced here: 438 us
  waiting for transfers between devices  301 us (68%)
  loops' own time  58.2 us (13%)
  local copies, waits for them, and re-layouts  36.9 us (8%)
  matrix products  18.1 us (4%)
  between operations  13.9 us (3%)
  other arithmetic  9.67 us (2%)
    psum x1, waiting for transfers between devices, shards(): lax.psum(head_term.astype(jnp.bfloat16), 'mp').astype(jnp.float32)  137 us
    all_gather x1, waiting for transfers between devices, shards(): shard_piece = lax.all_gather(prefix_kv, 'req', axis=1, tiled=True)  103 us
    reduce_scatter x1, waiting for transfers between devices, shards(): lax.psum_scatter(projected.astype(jnp.bfloat16), 'mp', scatter_dimension=...  60.8 us
    another operation x1, loops' own time, shards(): result = lax.fori_loop(0, block_total, fold_step, own_part)  50.1 us
    reshape x1, local copies, waits for them, and re-layouts, shards(): blocks_here = shard_piece.reshape(2, block_total, KB, head_count, DH)  12.5 us
    unnamed x17, local copies, waits for them, and re-layouts  11.3 us
    dynamic_slice x16, local copies, waits for them, and re-layouts, fold_step(): logical = prefix_owner[block_index]  9.59 us
  transfers between devices with their start and end apart: 3, of which 3 were waited for; matrix products, arithmetic and copies ran while one was open for 2% of the time, Pallas kernels for 0%

commit v1 on v0

v1 whole, which is shorter than its diff:
```python
import functools

import jax
import jax.numpy as jnp
from jax import lax
from jax.experimental import pallas as pl
from jax.experimental.pallas import tpu as pltpu
from jax.sharding import PartitionSpec as P

MESH = pl.DeviceIdType.MESH
H = 32
DH = 128
KB = 512
S_MAX = 128
P_SIZE = 2048
PER_GROUP = P_SIZE // KB
NX = 4
NZH = 4
NY = 4
NZL = 2
NCHIP = NY * NZL
NREQ = NX * NZH
NEG = -1e30
ROWS = S_MAX
COLS = 2 * DH
D = 4096
HALF = D // 2
UNITS = 512
STAT = 16
SLOT = COLS + STAT

Z_FAR = (2, 1, 3)
X_NEAR = (1, 3, 2)
CHIPS = ((1, 2), (1, 1), (1, 3), (0, 2), (1, 0), (0, 1), (0, 3))

F32 = jnp.float32
BF16 = jnp.bfloat16


def nt(a, b):
    return lax.dot_general(a, b, (((1,), (1,)), ((), ())), preferred_element_type=F32)


def nn(a, b):
    return lax.dot_general(a, b, (((1,), (0,)), ((), ())), preferred_element_type=F32)


def slope_of(head):
    k = head + 1
    whole, part = k // 4, lax.rem(k, 4)
    out = jnp.float32(1.0)
    for i in range(1, 9):
        out = jnp.where(whole == i, jnp.float32(2.0**-i), out)
    frac = jnp.float32(1.0)
    for i in range(1, 4):
        frac = jnp.where(part == i, jnp.float32(2.0 ** (-0.25 * i)), frac)
    return out * frac


def split3(v):
    hi = v.astype(BF16).astype(F32)
    rest = v - hi
    mid = rest.astype(BF16).astype(F32)
    return hi, mid, rest - mid


def pack_stats(ms, ls):
    row = lax.broadcasted_iota(jnp.int32, (STAT, ROWS), 0)
    out = jnp.zeros((STAT, ROWS), F32)
    at = 0
    for m, l in zip(ms, ls):
        for part in split3(m) + split3(l):
            out = jnp.where(row == at, part, out)
            at += 1
    return out.astype(BF16)


def unpack_stats(block):
    st = block.astype(F32)
    ms, ls = [], []
    for h in range(2):
        at = 6 * h
        ms.append(st[at : at + 1] + st[at + 1 : at + 2] + st[at + 2 : at + 3])
        ls.append(st[at + 3 : at + 4] + st[at + 4 : at + 5] + st[at + 5 : at + 6])
    return ms, ls


def combine(parts):
    ms, ls, os = [], [], []
    for h in range(2):
        m = parts[0][0][h]
        for part in parts[1:]:
            m = jnp.maximum(m, part[0][h])
        l, o = None, None
        for part in parts:
            scale = jnp.exp(part[0][h] - m)
            pl_, po = part[1][h] * scale, part[2][h] * scale
            l = pl_ if l is None else l + pl_
            o = po if o is None else o + po
        ms.append(m)
        ls.append(l)
        os.append(o)
    return ms, ls, os


def read_slot(ref, lead):
    ms, ls = unpack_stats(ref[lead + (pl.ds(COLS, STAT), slice(None))])
    os = [ref[lead + (pl.ds(h * DH, DH), slice(None))].astype(F32) for h in range(2)]
    return ms, ls, os


def erf(x):
    return lax.erf(x)


def kernel(
    len_ref,
    grp_ref,
    own_ref,
    q_hbm,
    skv_hbm,
    pkv_hbm,
    res_hbm,
    gain_hbm,
    ow_hbm,
    uw_hbm,
    dw_hbm,
    att_out,
    lay_out,
    qall,
    qv,
    skv,
    pkv,
    res,
    gain,
    ow,
    uw,
    dw,
    vt,
    sufo,
    sufs,
    obuf,
    sendb,
    xrecv,
    zsend,
    zrecv,
    respad,
    pre_s,
    pre_r,
    rs_s,
    rs_r,
    st_s,
    st_r,
    mixed,
    nall,
    tmp,
    pre2_s,
    pre2_r,
    rs2_s,
    rs2_r,
    loc,
    qzs,
    qxs,
    qrs,
    pxs,
    pxr,
    pzs,
    pzr,
    p1s,
    p1r,
    r1s,
    r1r,
    sts,
    strv,
    ags,
    agr,
    fws,
    fwr,
    p2s,
    p2r,
    r2s,
    r2r,
):
    me_r = lax.axis_index("req")
    me_m = lax.axis_index("mp")
    zh, x = me_r // NX, lax.rem(me_r, NX)
    core = lax.rem(me_m, 2)
    chip = me_m // 2
    zl, y = chip // NY, lax.rem(chip, NY)
    other = 1 - core

    def req_at(dz, dx):
        return lax.rem(zh + dz, NZH) * NX + lax.rem(x + dx, NX)

    def req_dev(dz, dx):
        return (req_at(dz, dx), me_m)

    def chip_at(off):
        return lax.rem(zl + off[0], NZL) * NY + lax.rem(y + off[1], NY)

    def back(off):
        return lax.rem(zl + off[0], NZL) * NY + lax.rem(y + NY - off[1], NY)

    def chip_dev(off):
        return (me_r, chip_at(off) * 2 + core)

    partner = (me_r, chip * 2 + other)
    sends = []

    def send(src, dst, ssem, rsem, dev):
        cp = pltpu.make_async_remote_copy(
            src_ref=src, dst_ref=dst, send_sem=ssem, recv_sem=rsem, device_id=dev, device_id_type=MESH
        )
        cp.start()
        sends.append(cp)

    def arrive(dst, ssem, rsem):
        pltpu.make_async_remote_copy(
            src_ref=dst, dst_ref=dst, send_sem=ssem, recv_sem=rsem, device_id=partner, device_id_type=MESH
        ).wait_recv()

    loads = {}
    for i, (name, src, dst) in enumerate(
        (
            ("q", q_hbm, qv),
            ("qa", q_hbm, qall.at[me_r]),
            ("skv", skv_hbm, skv),
            ("pkv", pkv_hbm, pkv),
            ("res", res_hbm, res),
            ("gain", gain_hbm, gain),
            ("ow", ow_hbm, ow),
            ("uw", uw_hbm, uw),
            ("dw", dw_hbm, dw),
        )
    ):
        loads[name] = pltpu.make_async_copy(src, dst, loc.at[i])
        loads[name].start()

    barrier = pltpu.get_barrier_semaphore()
    peers = [req_dev(d, 0) for d in Z_FAR] + [req_dev(0, d) for d in X_NEAR]
    peers += [chip_dev(o) for o in CHIPS] + [partner]
    for dev in peers:
        pl.semaphore_signal(barrier, inc=1, device_id=dev, device_id_type=MESH)
    pl.semaphore_wait(barrier, len(peers))

    for i, d in enumerate(Z_FAR):
        send(q_hbm, qall.at[me_r], qzs.at[i], qrs.at[me_r], req_dev(d, 0))
    for i, d in enumerate(X_NEAR):
        send(q_hbm, qall.at[me_r], qxs.at[0, i], qrs.at[me_r], req_dev(0, d))

    my_len = len_ref[me_r]
    slopes = [slope_of(2 * me_m + h) for h in range(2)]
    scale = float(DH) ** (-0.5)
    loads["q"].wait()
    loads["skv"].wait()
    key_i = lax.broadcasted_iota(jnp.int32, (S_MAX, ROWS), 0)
    slot_i = lax.broadcasted_iota(jnp.int32, (S_MAX, ROWS), 1)
    allowed = (key_i <= slot_i) & (key_i < my_len)
    gap = (slot_i - key_i).astype(F32)
    for h in range(2):
        cols = slice(h * DH, (h + 1) * DH)
        s = nt(skv[0, :, cols], qv[:, cols]) * scale - slopes[h] * gap
        s = jnp.where(allowed, s, NEG)
        m = jnp.max(s, axis=0, keepdims=True)
        w = jnp.where(allowed, jnp.exp(s - m), 0.0)
        sufs[2 * h : 2 * h + 1, :] = m
        sufs[2 * h + 1 : 2 * h + 2, :] = jnp.sum(w, axis=0, keepdims=True)
        sufo[h] = nn(skv[1, :, cols].T, w.astype(BF16))
    loads["pkv"].wait()
    for h in range(2):
        vt[h] = pkv[1, :, h * DH : (h + 1) * DH].T

    for j, d in enumerate((1, 3, 2)):
        src = req_at(d, 0)
        arrive(qall.at[src], qzs.at[0], qrs.at[src])
        for i, dx in enumerate(X_NEAR):
            send(qall.at[src], qall.at[src], qxs.at[1 + j, i], qrs.at[src], req_dev(0, dx))

    logical = own_ref[me_r]
    group = logical // PER_GROUP
    base = (logical - group * PER_GROUP) * KB
    picks = [jnp.int32(0)] * 4
    sel = []
    seen = jnp.int32(0)
    for r in range(NREQ):
        hit = grp_ref[r] == group
        for j in range(4):
            picks[j] = jnp.where(hit & (seen == j), jnp.int32(r), picks[j])
        sel.append(jnp.where(hit, jnp.minimum(seen, 3), 4))
        seen = seen + jnp.where(hit, 1, 0)
    obuf[4] = jnp.concatenate(
        [
            jnp.zeros((COLS, ROWS), BF16),
            pack_stats([jnp.full((1, ROWS), NEG, F32)] * 2, [jnp.zeros((1, ROWS), F32)] * 2),
        ],
        axis=0,
    )

    loads["qa"].wait()
    for dz in (0, 1, 3, 2):
        for dx in X_NEAR:
            src = req_at(dz, dx)
            arrive(qall.at[src], qzs.at[0], qrs.at[src])

    pkey = lax.broadcasted_iota(jnp.int32, (KB, ROWS), 0)
    pslot = lax.broadcasted_iota(jnp.int32, (KB, ROWS), 1)
    dist = (P_SIZE - base + pslot - pkey).astype(F32)
    for j in range(4):
        ms, ls = [], []
        for h in range(2):
            cols = slice(h * DH, (h + 1) * DH)
            s = nt(pkv[0, :, cols], qall[picks[j], :, cols]) * scale - slopes[h] * dist
            m = jnp.max(s, axis=0, keepdims=True)
            w = jnp.exp(s - m)
            ms.append(m)
            ls.append(jnp.sum(w, axis=0, keepdims=True))
            obuf[j, cols, :] = nn(vt[h], w.astype(BF16)).astype(BF16)
        obuf[j, COLS:SLOT, :] = pack_stats(ms, ls)
    for r in range(NREQ):
        sendb[r] = obuf[sel[r]]

    for dz in (2, 1, 3, 0):
        for i, dx in enumerate(X_NEAR):
            send(sendb.at[req_at(dz, dx)], xrecv.at[dx - 1, dz], pxs.at[dx - 1, dz], pxr.at[dx - 1, dz], req_dev(0, dx))
    final = None
    for dz in (2, 1, 3, 0):
        parts = [read_slot(sendb, (req_at(dz, 0),))]
        for dx in X_NEAR:
            arrive(xrecv.at[dx - 1, dz], pxs.at[dx - 1, dz], pxr.at[dx - 1, dz])
            parts.append(read_slot(xrecv, (dx - 1, dz)))
        if dz == 0:
            parts.append(
                (
                    [sufs[0:1, :], sufs[2:3, :]],
                    [sufs[1:2, :], sufs[3:4, :]],
                    [sufo[0], sufo[1]],
                )
            )
        ms, ls, os = combine(parts)
        if dz == 0:
            final = (ms, ls, os)
        else:
            for h in range(2):
                zsend[dz - 1, h * DH : (h + 1) * DH, :] = os[h].astype(BF16)
            zsend[dz - 1, COLS:SLOT, :] = pack_stats(ms, ls)
            send(zsend.at[dz - 1], zrecv.at[dz - 1], pzs.at[dz - 1], pzr.at[dz - 1], req_dev(dz, 0))
    parts = [final]
    for dz in (1, 3, 2):
        arrive(zrecv.at[dz - 1], pzs.at[dz - 1], pzr.at[dz - 1])
        parts.append(read_slot(zrecv, (dz - 1,)))
    ms, ls, os = combine(parts)
    live = lax.broadcasted_iota(jnp.int32, (DH, ROWS), 1) < my_len
    for h in range(2):
        att_out[:, h * DH : (h + 1) * DH] = jnp.where(live, os[h] / ls[h], 0.0).T.astype(BF16)

    loads["res"].wait()
    loads["ow"].wait()
    respad[...] = jnp.zeros_like(respad)
    respad[:, pl.ds(pl.multiple_of(core * COLS, COLS), COLS)] = res[...].astype(F32)
    wide = 512

    def head_term(half, n):
        at = pl.multiple_of(half * HALF + n * wide, wide)
        t = nn(att_out[...], ow[:, pl.ds(at, wide)])
        return t + jnp.where(half * (HALF // wide) + n == chip, respad[...], 0.0)

    for n in range(HALF // wide):
        pre_s[n] = head_term(other, n).astype(BF16)
        send(pre_s.at[n], pre_r.at[n], p1s.at[n], p1r.at[n], partner)
    for n in range(HALF // wide):
        t = head_term(core, n)
        arrive(pre_r.at[n], p1s.at[n], p1r.at[n])
        rs_s[:, n * wide : (n + 1) * wide] = (t + pre_r[n].astype(F32)).astype(BF16)
    for i, off in enumerate(CHIPS):
        rows = pl.ds(pl.multiple_of(chip_at(off) * 16, 16), 16)
        send(rs_s.at[rows], rs_r.at[i], r1s.at[i], r1r.at[i], chip_dev(off))
    my_rows = pl.ds(pl.multiple_of(chip * 16, 16), 16)
    tot = rs_s[my_rows, :].astype(F32)
    for i in reversed(range(len(CHIPS))):
        arrive(rs_r.at[i], r1s.at[i], r1r.at[i])
        tot = tot + rs_r[i].astype(F32)

    mean_a = jnp.sum(tot, axis=1, keepdims=True) * (1.0 / HALF)
    cent = tot - mean_a
    m2_a = jnp.sum(cent * cent, axis=1, keepdims=True)
    lane = lax.broadcasted_iota(jnp.int32, (16, 128), 1)
    st_s[...] = jnp.where(lane < 64, mean_a, m2_a)
    send(st_s, st_r, sts.at[0], strv.at[0], partner)
    mixed[...] = tot
    loads["gain"].wait()
    arrive(st_r, sts.at[0], strv.at[0])
    mean_b, m2_b = st_r[:, 0:1], st_r[:, 64:65]
    diff = mean_a - mean_b
    mean = 0.5 * (mean_a + mean_b)
    var = (m2_a + m2_b + diff * diff * (HALF / 2)) * (1.0 / D)
    my_gain = gain[0:1, pl.ds(pl.multiple_of(core * HALF, HALF), HALF)]
    nall[core, my_rows, :] = ((tot - mean) * lax.rsqrt(var + 1e-05) * my_gain).astype(BF16)
    for i, off in enumerate(CHIPS):
        send(nall.at[core, my_rows], nall.at[core, my_rows], ags.at[i], agr.at[i], chip_dev(off))
    send(nall.at[core, my_rows], nall.at[core, my_rows], fws.at[7], fwr.at[7], partner)
    for i in reversed(range(len(CHIPS))):
        rows = pl.ds(pl.multiple_of(back(CHIPS[i]) * 16, 16), 16)
        arrive(nall.at[core, rows], ags.at[i], agr.at[i])
        send(nall.at[core, rows], nall.at[core, rows], fws.at[i], fwr.at[i], partner)

    loads["uw"].wait()
    acc = nn(nall[core], uw[pl.ds(pl.multiple_of(core * HALF, HALF), HALF), :])
    for i in range(len(CHIPS)):
        rows = pl.ds(pl.multiple_of(back(CHIPS[i]) * 16, 16), 16)
        arrive(nall.at[other, rows], fws.at[i], fwr.at[i])
    arrive(nall.at[other, my_rows], fws.at[7], fwr.at[7])
    acc = acc + nn(nall[other], uw[pl.ds(pl.multiple_of(other * HALF, HALF), HALF), :])
    hid = (acc * (0.5 * (1.0 + erf(acc * (0.5**0.5))))).astype(BF16)

    loads["dw"].wait()
    order = CHIPS + ((0, 0),)

    def unit_term(off, which):
        block = chip_at(off) * 2 + which
        t = nn(hid, dw[:, pl.ds(pl.multiple_of(block * COLS, COLS), COLS)])
        inner = lax.rem(block, NCHIP)
        add = mixed[:, pl.ds(pl.multiple_of(inner * COLS, COLS), COLS)]
        tmp[...] = t
        tmp[my_rows, :] = tmp[my_rows, :] + jnp.where(block // NCHIP == core, add, 0.0)
        return tmp[...]

    for i, off in enumerate(order):
        pre2_s[i] = unit_term(off, other).astype(BF16)
        send(pre2_s.at[i], pre2_r.at[i], p2s.at[i], p2r.at[i], partner)
    out = None
    for i, off in enumerate(order):
        t = unit_term(off, core)
        arrive(pre2_r.at[i], p2s.at[i], p2r.at[i])
        t = t + pre2_r[i].astype(F32)
        if i < len(CHIPS):
            rs2_s[i] = t.astype(BF16)
            send(rs2_s.at[i], rs2_r.at[i], r2s.at[i], r2r.at[i], chip_dev(off))
        else:
            out = t
    for i in reversed(range(len(CHIPS))):
        arrive(rs2_r.at[i], r2s.at[i], r2r.at[i])
        out = out + rs2_r[i].astype(F32)
    row_live = lax.broadcasted_iota(jnp.int32, (ROWS, COLS), 0) < my_len
    lay_out[...] = jnp.where(row_live, out, 0.0).astype(BF16)
    for cp in sends:
        cp.wait_send()


def shards(
    queries,
    suffix_kv,
    prefix_kv,
    resid,
    ln_gain,
    out_weight,
    up_weight,
    down_weight,
    lengths,
    req_group,
    prefix_owner,
):
    smem = pl.BlockSpec(memory_space=pltpu.SMEM)
    anym = pl.BlockSpec(memory_space=pl.ANY)
    vmem = pl.BlockSpec(memory_space=pltpu.VMEM)
    dma = pltpu.SemaphoreType.DMA
    vm = pltpu.VMEM
    n = HALF // 512
    nc = len(CHIPS)
    return pl.pallas_call(
        kernel,
        out_shape=[jax.ShapeDtypeStruct((ROWS, COLS), BF16)] * 2,
        in_specs=[smem] * 3 + [anym] * 8,
        out_specs=[vmem] * 2,
        scratch_shapes=[
            vm((NREQ, ROWS, COLS), BF16),
            vm((ROWS, COLS), BF16),
            vm((2, S_MAX, COLS), BF16),
            vm((2, KB, COLS), BF16),
            vm((ROWS, COLS), BF16),
            vm((1, D), F32),
            vm((COLS, D), BF16),
            vm((D, UNITS), BF16),
            vm((UNITS, D), BF16),
            vm((2, DH, KB), BF16),
            vm((2, DH, ROWS), F32),
            vm((8, ROWS), F32),
            vm((5, SLOT, ROWS), BF16),
            vm((NREQ, SLOT, ROWS), BF16),
            vm((3, NZH, SLOT, ROWS), BF16),
            vm((3, SLOT, ROWS), BF16),
            vm((3, SLOT, ROWS), BF16),
            vm((ROWS, 512), F32),
            vm((n, ROWS, 512), BF16),
            vm((n, ROWS, 512), BF16),
            vm((ROWS, HALF), BF16),
            vm((nc, 16, HALF), BF16),
            vm((16, 128), F32),
            vm((16, 128), F32),
            vm((16, HALF), F32),
            vm((2, ROWS, HALF), BF16),
            vm((ROWS, COLS), F32),
            vm((8, ROWS, COLS), BF16),
            vm((8, ROWS, COLS), BF16),
            vm((nc, ROWS, COLS), BF16),
            vm((nc, ROWS, COLS), BF16),
            dma((9,)),
            dma((3,)),
            dma((4, 3)),
            dma((NREQ,)),
            dma((3, NZH)),
            dma((3, NZH)),
            dma((3,)),
            dma((3,)),
            dma((n,)),
            dma((n,)),
            dma((nc,)),
            dma((nc,)),
            dma((1,)),
            dma((1,)),
            dma((nc,)),
            dma((nc,)),
            dma((8,)),
            dma((8,)),
            dma((8,)),
            dma((8,)),
            dma((nc,)),
            dma((nc,)),
        ],
        compiler_params=pltpu.CompilerParams(
            collective_id=0, has_side_effects=True, vmem_limit_bytes=56 * 2**20
        ),
        name="prefill_layer",
    )(
        lengths,
        req_group,
        prefix_owner,
        queries,
        suffix_kv,
        prefix_kv,
        resid,
        ln_gain.reshape(1, D),
        out_weight,
        up_weight,
        down_weight,
    )


def solution(mesh):
    placed = (
        P("req", "mp"),
        P(None, "req", "mp"),
        P(None, "req", "mp"),
        P("req", "mp"),
        P(),
        P("mp", None),
        P(None, "mp"),
        P("mp", None),
        P(),
        P(),
        P(),
    )
    return jax.shard_map(
        shards,
        mesh=mesh,
        in_specs=placed,
        out_specs=(P("req", "mp"), P("req", "mp")),
        check_vma=False,
    )
```

time: 442 us -> 84.6 us (0.19)
  waiting for transfers between devices: 301 us -> 0 us
  Pallas kernels: 0 us -> 80.9 us
  loops' own time: 58.2 us -> 0 us
  local copies, waits for them, and re-layouts: 36.9 us -> 2.95 us
  matrix products: 18.1 us -> 0 us
  between operations: 13.9 us -> 0.64 us
  other arithmetic: 9.67 us -> 0 us
    psum x1 -> x0, waiting for transfers between devices: 137 us -> none  [shards(): lax.psum(head_term.astype(jnp.bfloat16), 'mp').astype(jnp.float32)]
    all_gather x1 -> x0, waiting for transfers between devices: 103 us -> none  [shards(): shard_piece = lax.all_gather(prefix_kv, 'req', axis=1, tiled=True)]
    pallas_call x0 -> x1, Pallas kernels: none -> 80.9 us  [shards(): pl.pallas_call(kernel, out_shape=[jax.ShapeDtypeStruct((ROWS, COLS), BF16...]
    reduce_scatter x1 -> x0, waiting for transfers between devices: 60.8 us -> none  [shards(): lax.psum_scatter(projected.astype(jnp.bfloat16), 'mp', scatter_dimension=...]
    another operation x17 -> x0, loops' own time: 58.2 us -> none  [the longest x1 50.1 us: shards(): result = lax.fori_loop(0, block_total, fold_step, own_part)]
    dot_general x12 -> x0, matrix products: 18.1 us -> none  [the longest x1 6.43 us: shards(): projected = jnp.dot(hidden, down_weight, preferred_element_type=jnp.float32)]
    reshape x1 -> x0, local copies, waits for them, and re-layouts: 12.5 us -> none  [shards(): blocks_here = shard_piece.reshape(2, block_total, KB, head_count, DH)]
    dynamic_slice x18 -> x0, local copies, waits for them, and re-layouts: 12 us -> none  [the longest x16 9.59 us: fold_step(): logical = prefix_owner[block_index]]
  transfers between devices with their start and end apart: 3 -> 0, of which waited for: 3 -> 0; matrix products, arithmetic and copies ran while one was open for 2% -> 0% of each run, Pallas kernels for 0% -> 0%
where the time goes in v1:
time: 84.6 us; the launch traced here: 84.5 us
  Pallas kernels  80.9 us (96%)
  local copies, waits for them, and re-layouts  2.95 us (3%)
    pallas_call x1, Pallas kernels, shards(): pl.pallas_call(kernel, out_shape=[jax.ShapeDtypeStruct((ROWS, COLS), BF16...  80.9 us
    unnamed x2, local copies, waits for them, and re-layouts  2.95 us

profile of v1, /device:TPU:1, one launch (start us, length us, event | category | flops | bytes accessed | tf_op | source)
XLA Modules:
  0.0 84.5 jit_solution(13681098336535465055)
XLA Ops:
  0.6 80.9 %prefill_layer.1 = (bf16[128,256]{1,0:T(8,128)(2,1)}, bf16[128,256]{1,0:T(8,128)(2,1)}) custom-call(s32[16]{0:T(128)} %len_ref.1, s32[16]{0:T(128)} %grp_ref.1, s32[16]{0:T(128)} %own_ref.1, bf16[128,256]{1,0:T(8,128)(2,1)} %q_hbm.1, bf16[2,128,256]{2,1,0:T(8,128)(2,1)} %skv_hbm.1, bf16[2,512,256]{2,1,0:T(8,128)(2,1)} %pkv_hbm.1, bf16[128,256]{1,0:T(8,128)(2,1)} %res_hbm.1, ...), custom_call_target="tpu_custom_call" | custom-call | tf_op jit(solution)/shard_map/prefill_layer/pallas_call | solution.py:469
  81.5 1.5 %copy.15 = bf16[128,256]{1,0:T(8,128)(2,1)} copy(bf16[128,256]{1,0:T(8,128)(2,1)} %get-tuple-element.4) | data formatting | bytes 131072
  83.0 1.5 %copy.16 = bf16[128,256]{1,0:T(8,128)(2,1)} copy(bf16[128,256]{1,0:T(8,128)(2,1)} %get-tuple-element.5) | data formatting | bytes 131072

commit v2 on v1

--- a/solution.py
+++ b/solution.py
@@ -30,7 +30,6 @@
 SLOT = COLS + STAT
 
 Z_FAR = (2, 1, 3)
-X_NEAR = (1, 3, 2)
 CHIPS = ((1, 2), (1, 1), (1, 3), (0, 2), (1, 0), (0, 1), (0, 3))
 
 F32 = jnp.float32
@@ -127,10 +126,9 @@
     dw_hbm,
     att_out,
     lay_out,
-    qall,
-    qv,
+    qz,
     skv,
-    pkv,
+    kvb,
     res,
     gain,
     ow,
@@ -139,9 +137,8 @@
     vt,
     sufo,
     sufs,
-    obuf,
-    sendb,
-    xrecv,
+    acco,
+    accs,
     zsend,
     zrecv,
     respad,
@@ -160,10 +157,9 @@
     rs2_r,
     loc,
     qzs,
-    qxs,
-    qrs,
-    pxs,
-    pxr,
+    qzr,
+    kvs,
+    kvr,
     pzs,
     pzr,
     p1s,
@@ -222,10 +218,9 @@
     loads = {}
     for i, (name, src, dst) in enumerate(
         (
-            ("q", q_hbm, qv),
-            ("qa", q_hbm, qall.at[me_r]),
+            ("q", q_hbm, qz.at[0]),
             ("skv", skv_hbm, skv),
-            ("pkv", pkv_hbm, pkv),
+            ("pkv", pkv_hbm, kvb.at[0]),
             ("res", res_hbm, res),
             ("gain", gain_hbm, gain),
             ("ow", ow_hbm, ow),
@@ -237,16 +232,22 @@
         loads[name].start()
 
     barrier = pltpu.get_barrier_semaphore()
-    peers = [req_dev(d, 0) for d in Z_FAR] + [req_dev(0, d) for d in X_NEAR]
+    peers = [req_dev(d, 0) for d in Z_FAR] + [req_dev(0, d) for d in (1, 3)]
     peers += [chip_dev(o) for o in CHIPS] + [partner]
     for dev in peers:
         pl.semaphore_signal(barrier, inc=1, device_id=dev, device_id_type=MESH)
     pl.semaphore_wait(barrier, len(peers))
 
+    right, left = req_dev(0, 1), req_dev(0, 3)
     for i, d in enumerate(Z_FAR):
-        send(q_hbm, qall.at[me_r], qzs.at[i], qrs.at[me_r], req_dev(d, 0))
-    for i, d in enumerate(X_NEAR):
-        send(q_hbm, qall.at[me_r], qxs.at[0, i], qrs.at[me_r], req_dev(0, d))
+        send(q_hbm, qz.at[4 - d], qzs.at[d - 1], qzr.at[3 - d], req_dev(d, 0))
+    send(pkv_hbm.at[0], kvb.at[3, 0], kvs.at[0, 0], kvr.at[3, 0], right)
+    send(pkv_hbm.at[1], kvb.at[1, 1], kvs.at[1, 0], kvr.at[1, 1], left)
+    send(pkv_hbm.at[1], kvb.at[3, 1], kvs.at[0, 1], kvr.at[3, 1], right)
+    send(pkv_hbm.at[0], kvb.at[1, 0], kvs.at[1, 1], kvr.at[1, 0], left)
+
+    def arrive_kv(dx, part):
+        arrive(kvb.at[dx, part], kvs.at[0, 0], kvr.at[dx, part])
 
     my_len = len_ref[me_r]
     slopes = [slope_of(2 * me_m + h) for h in range(2)]
@@ -259,92 +260,82 @@
     gap = (slot_i - key_i).astype(F32)
     for h in range(2):
         cols = slice(h * DH, (h + 1) * DH)
-        s = nt(skv[0, :, cols], qv[:, cols]) * scale - slopes[h] * gap
+        s = nt(skv[0, :, cols], qz[0, :, cols]) * scale - slopes[h] * gap
         s = jnp.where(allowed, s, NEG)
         m = jnp.max(s, axis=0, keepdims=True)
         w = jnp.where(allowed, jnp.exp(s - m), 0.0)
         sufs[2 * h : 2 * h + 1, :] = m
         sufs[2 * h + 1 : 2 * h + 2, :] = jnp.sum(w, axis=0, keepdims=True)
         sufo[h] = nn(skv[1, :, cols].T, w.astype(BF16))
-    loads["pkv"].wait()
-    for h in range(2):
-        vt[h] = pkv[1, :, h * DH : (h + 1) * DH].T
-
-    for j, d in enumerate((1, 3, 2)):
-        src = req_at(d, 0)
-        arrive(qall.at[src], qzs.at[0], qrs.at[src])
-        for i, dx in enumerate(X_NEAR):
-            send(qall.at[src], qall.at[src], qxs.at[1 + j, i], qrs.at[src], req_dev(0, dx))
-
-    logical = own_ref[me_r]
-    group = logical // PER_GROUP
-    base = (logical - group * PER_GROUP) * KB
-    picks = [jnp.int32(0)] * 4
-    sel = []
-    seen = jnp.int32(0)
-    for r in range(NREQ):
-        hit = grp_ref[r] == group
-        for j in range(4):
-            picks[j] = jnp.where(hit & (seen == j), jnp.int32(r), picks[j])
-        sel.append(jnp.where(hit, jnp.minimum(seen, 3), 4))
-        seen = seen + jnp.where(hit, 1, 0)
-    obuf[4] = jnp.concatenate(
-        [
-            jnp.zeros((COLS, ROWS), BF16),
-            pack_stats([jnp.full((1, ROWS), NEG, F32)] * 2, [jnp.zeros((1, ROWS), F32)] * 2),
-        ],
-        axis=0,
-    )
-
-    loads["qa"].wait()
-    for dz in (0, 1, 3, 2):
-        for dx in X_NEAR:
-            src = req_at(dz, dx)
-            arrive(qall.at[src], qzs.at[0], qrs.at[src])
+
+    arrive_kv(3, 0)
+    send(kvb.at[3, 0], kvb.at[2, 0], kvs.at[0, 2], kvr.at[2, 0], right)
+    arrive_kv(1, 1)
+    send(kvb.at[1, 1], kvb.at[2, 1], kvs.at[1, 2], kvr.at[2, 1], left)
 
     pkey = lax.broadcasted_iota(jnp.int32, (KB, ROWS), 0)
     pslot = lax.broadcasted_iota(jnp.int32, (KB, ROWS), 1)
-    dist = (P_SIZE - base + pslot - pkey).astype(F32)
-    for j in range(4):
-        ms, ls = [], []
+    loads["pkv"].wait()
+    for d in (1, 3, 2):
+        arrive(qz.at[d], qzs.at[0], qzr.at[d - 1])
+
+    def block_part(dx, dz):
+        logical = own_ref[req_at(0, dx)]
+        group = logical // PER_GROUP
+        base = (logical - group * PER_GROUP) * KB
+        valid = grp_ref[req_at(dz, 0)] == group
+        dist = (P_SIZE - base + pslot - pkey).astype(F32)
+        ms, ls, os = [], [], []
         for h in range(2):
             cols = slice(h * DH, (h + 1) * DH)
-            s = nt(pkv[0, :, cols], qall[picks[j], :, cols]) * scale - slopes[h] * dist
+            s = nt(kvb[dx, 0, :, cols], qz[dz, :, cols]) * scale - slopes[h] * dist
             m = jnp.max(s, axis=0, keepdims=True)
             w = jnp.exp(s - m)
-            ms.append(m)
+            ms.append(jnp.where(valid, m, NEG))
             ls.append(jnp.sum(w, axis=0, keepdims=True))
-            obuf[j, cols, :] = nn(vt[h], w.astype(BF16)).astype(BF16)
-        obuf[j, COLS:SLOT, :] = pack_stats(ms, ls)
-    for r in range(NREQ):
-        sendb[r] = obuf[sel[r]]
-
-    for dz in (2, 1, 3, 0):
-        for i, dx in enumerate(X_NEAR):
-            send(sendb.at[req_at(dz, dx)], xrecv.at[dx - 1, dz], pxs.at[dx - 1, dz], pxr.at[dx - 1, dz], req_dev(0, dx))
-    final = None
-    for dz in (2, 1, 3, 0):
-        parts = [read_slot(sendb, (req_at(dz, 0),))]
-        for dx in X_NEAR:
-            arrive(xrecv.at[dx - 1, dz], pxs.at[dx - 1, dz], pxr.at[dx - 1, dz])
-            parts.append(read_slot(xrecv, (dx - 1, dz)))
-        if dz == 0:
-            parts.append(
-                (
-                    [sufs[0:1, :], sufs[2:3, :]],
-                    [sufs[1:2, :], sufs[3:4, :]],
-                    [sufo[0], sufo[1]],
-                )
-            )
-        ms, ls, os = combine(parts)
-        if dz == 0:
-            final = (ms, ls, os)
-        else:
-            for h in range(2):
-                zsend[dz - 1, h * DH : (h + 1) * DH, :] = os[h].astype(BF16)
-            zsend[dz - 1, COLS:SLOT, :] = pack_stats(ms, ls)
-            send(zsend.at[dz - 1], zrecv.at[dz - 1], pzs.at[dz - 1], pzr.at[dz - 1], req_dev(dz, 0))
-    parts = [final]
+            os.append(nn(vt[h], w.astype(BF16)))
+        return ms, ls, os
+
+    def held(dz):
+        at = 4 * dz
+        return (
+            [accs[at + 2 * h : at + 2 * h + 1, :] for h in range(2)],
+            [accs[at + 2 * h + 1 : at + 2 * h + 2, :] for h in range(2)],
+            [acco[dz, h] for h in range(2)],
+        )
+
+    def hold(dz, part):
+        at = 4 * dz
+        for h in range(2):
+            accs[at + 2 * h : at + 2 * h + 1, :] = part[0][h]
+            accs[at + 2 * h + 1 : at + 2 * h + 2, :] = part[1][h]
+            acco[dz, h] = part[2][h]
+
+    for dx in (0, 1, 3, 2):
+        if dx == 1:
+            arrive_kv(1, 0)
+        if dx == 3:
+            arrive_kv(3, 1)
+        if dx == 2:
+            arrive_kv(2, 0)
+            arrive_kv(2, 1)
+        for h in range(2):
+            vt[h] = kvb[dx, 1, :, h * DH : (h + 1) * DH].T
+        for dz in (2, 1, 3, 0):
+            part = block_part(dx, dz)
+            if dx != 0:
+                part = combine([held(dz), part])
+            if dx != 2 or dz == 0:
+                hold(dz, part)
+            else:
+                ms, ls, os = part
+                for h in range(2):
+                    zsend[dz - 1, h * DH : (h + 1) * DH, :] = os[h].astype(BF16)
+                zsend[dz - 1, COLS:SLOT, :] = pack_stats(ms, ls)
+                send(zsend.at[dz - 1], zrecv.at[dz - 1], pzs.at[dz - 1], pzr.at[dz - 1], req_dev(dz, 0))
+
+    suffix = ([sufs[0:1, :], sufs[2:3, :]], [sufs[1:2, :], sufs[3:4, :]], [sufo[0], sufo[1]])
+    parts = [held(0), suffix]
     for dz in (1, 3, 2):
         arrive(zrecv.at[dz - 1], pzs.at[dz - 1], pzr.at[dz - 1])
         parts.append(read_slot(zrecv, (dz - 1,)))
@@ -472,10 +463,9 @@
         in_specs=[smem] * 3 + [anym] * 8,
         out_specs=[vmem] * 2,
         scratch_shapes=[
-            vm((NREQ, ROWS, COLS), BF16),
-            vm((ROWS, COLS), BF16),
+            vm((NZH, ROWS, COLS), BF16),
             vm((2, S_MAX, COLS), BF16),
-            vm((2, KB, COLS), BF16),
+            vm((NX, 2, KB, COLS), BF16),
             vm((ROWS, COLS), BF16),
             vm((1, D), F32),
             vm((COLS, D), BF16),
@@ -484,9 +474,8 @@
             vm((2, DH, KB), BF16),
             vm((2, DH, ROWS), F32),
             vm((8, ROWS), F32),
-            vm((5, SLOT, ROWS), BF16),
-            vm((NREQ, SLOT, ROWS), BF16),
-            vm((3, NZH, SLOT, ROWS), BF16),
+            vm((NZH, 2, DH, ROWS), F32),
+            vm((16, ROWS), F32),
             vm((3, SLOT, ROWS), BF16),
             vm((3, SLOT, ROWS), BF16),
             vm((ROWS, 512), F32),
@@ -503,12 +492,11 @@
             vm((8, ROWS, COLS), BF16),
             vm((nc, ROWS, COLS), BF16),
             vm((nc, ROWS, COLS), BF16),
-            dma((9,)),
+            dma((8,)),
             dma((3,)),
-            dma((4, 3)),
-            dma((NREQ,)),
-            dma((3, NZH)),
-            dma((3, NZH)),
+            dma((3,)),
+            dma((2, 3)),
+            dma((NX, 2)),
             dma((3,)),
             dma((3,)),
             dma((n,)),

time: 84.6 us -> 77.5 us (0.916)
  Pallas kernels: 80.9 us -> 73.8 us
    pallas_call x1, Pallas kernels: 80.9 us -> 73.8 us  [shards(): pl.pallas_call(kernel, out_shape=[jax.ShapeDtypeStruct((ROWS, COLS), BF16...]
where the time goes in v2:
time: 77.5 us; the launch traced here: 77.3 us
  Pallas kernels  73.8 us (95%)
  local copies, waits for them, and re-layouts  2.95 us (4%)
    pallas_call x1, Pallas kernels, shards(): pl.pallas_call(kernel, out_shape=[jax.ShapeDtypeStruct((ROWS, COLS), BF16...  73.8 us
    unnamed x2, local copies, waits for them, and re-layouts  2.95 us

profile of v2, /device:TPU:1, one launch (start us, length us, event | category | flops | bytes accessed | tf_op | source)
XLA Modules:
  0.0 77.3 jit_solution(6188302240637086422)
XLA Ops:
  0.6 73.8 %prefill_layer.1 = (bf16[128,256]{1,0:T(8,128)(2,1)}, bf16[128,256]{1,0:T(8,128)(2,1)}) custom-call(s32[16]{0:T(128)} %len_ref.1, s32[16]{0:T(128)} %grp_ref.1, s32[16]{0:T(128)} %own_ref.1, bf16[128,256]{1,0:T(8,128)(2,1)} %q_hbm.1, bf16[2,128,256]{2,1,0:T(8,128)(2,1)} %skv_hbm.1, bf16[2,512,256]{2,1,0:T(8,128)(2,1)} %pkv_hbm.1, bf16[128,256]{1,0:T(8,128)(2,1)} %res_hbm.1, ...), custom_call_target="tpu_custom_call" | custom-call | tf_op jit(solution)/shard_map/prefill_layer/pallas_call | solution.py:460
  74.4 1.5 %copy.15 = bf16[128,256]{1,0:T(8,128)(2,1)} copy(bf16[128,256]{1,0:T(8,128)(2,1)} %get-tuple-element.4) | data formatting | bytes 131072
  75.9 1.5 %copy.16 = bf16[128,256]{1,0:T(8,128)(2,1)} copy(bf16[128,256]{1,0:T(8,128)(2,1)} %get-tuple-element.5) | data formatting | bytes 131072

commit v3 on v2

--- a/solution.py
+++ b/solution.py
@@ -26,6 +26,7 @@
 D = 4096
 HALF = D // 2
 UNITS = 512
+HR = ROWS // 2
 STAT = 16
 SLOT = COLS + STAT
 
@@ -151,6 +152,7 @@
     mixed,
     nall,
     tmp,
+    outk,
     pre2_s,
     pre2_r,
     rs2_s,
@@ -350,89 +352,127 @@
     respad[:, pl.ds(pl.multiple_of(core * COLS, COLS), COLS)] = res[...].astype(F32)
     wide = 512
 
-    def head_term(half, n):
+    def head_term(half, n, rows):
         at = pl.multiple_of(half * HALF + n * wide, wide)
-        t = nn(att_out[...], ow[:, pl.ds(at, wide)])
-        return t + jnp.where(half * (HALF // wide) + n == chip, respad[...], 0.0)
-
-    for n in range(HALF // wide):
-        pre_s[n] = head_term(other, n).astype(BF16)
+        t = nn(att_out[rows, :], ow[:, pl.ds(at, wide)])
+        return t + jnp.where(half * (HALF // wide) + n == chip, respad[rows, :], 0.0)
+
+    def rows_of(a):
+        return slice(a * HR, (a + 1) * HR)
+
+    for n in (0, 2, 1, 3):
+        pre_s[n] = head_term(other, n, slice(None)).astype(BF16)
         send(pre_s.at[n], pre_r.at[n], p1s.at[n], p1r.at[n], partner)
-    for n in range(HALF // wide):
-        t = head_term(core, n)
-        arrive(pre_r.at[n], p1s.at[n], p1r.at[n])
-        rs_s[:, n * wide : (n + 1) * wide] = (t + pre_r[n].astype(F32)).astype(BF16)
-    for i, off in enumerate(CHIPS):
-        rows = pl.ds(pl.multiple_of(chip_at(off) * 16, 16), 16)
-        send(rs_s.at[rows], rs_r.at[i], r1s.at[i], r1r.at[i], chip_dev(off))
-    my_rows = pl.ds(pl.multiple_of(chip * 16, 16), 16)
-    tot = rs_s[my_rows, :].astype(F32)
-    for i in reversed(range(len(CHIPS))):
-        arrive(rs_r.at[i], r1s.at[i], r1r.at[i])
-        tot = tot + rs_r[i].astype(F32)
-
-    mean_a = jnp.sum(tot, axis=1, keepdims=True) * (1.0 / HALF)
-    cent = tot - mean_a
-    m2_a = jnp.sum(cent * cent, axis=1, keepdims=True)
-    lane = lax.broadcasted_iota(jnp.int32, (16, 128), 1)
-    st_s[...] = jnp.where(lane < 64, mean_a, m2_a)
-    send(st_s, st_r, sts.at[0], strv.at[0], partner)
-    mixed[...] = tot
+
+    for a in range(2):
+        for n in range(2):
+            terms = []
+            for cn in (n, n + 2):
+                t = head_term(core, cn, rows_of(a))
+                if a == 0:
+                    arrive(pre_r.at[cn], p1s.at[cn], p1r.at[cn])
+                terms.append(t + pre_r[cn, rows_of(a), :].astype(F32))
+            for k in range(NCHIP):
+                rs_s[a, k, :, n * wide : (n + 1) * wide] = jnp.concatenate(
+                    [t[8 * k : 8 * k + 8] for t in terms], axis=0
+                ).astype(BF16)
+        for i, off in enumerate(CHIPS):
+            send(rs_s.at[a, chip_at(off)], rs_r.at[a, i], r1s.at[a, i], r1r.at[a, i], chip_dev(off))
     loads["gain"].wait()
-    arrive(st_r, sts.at[0], strv.at[0])
-    mean_b, m2_b = st_r[:, 0:1], st_r[:, 64:65]
-    diff = mean_a - mean_b
-    mean = 0.5 * (mean_a + mean_b)
-    var = (m2_a + m2_b + diff * diff * (HALF / 2)) * (1.0 / D)
-    my_gain = gain[0:1, pl.ds(pl.multiple_of(core * HALF, HALF), HALF)]
-    nall[core, my_rows, :] = ((tot - mean) * lax.rsqrt(var + 1e-05) * my_gain).astype(BF16)
-    for i, off in enumerate(CHIPS):
-        send(nall.at[core, my_rows], nall.at[core, my_rows], ags.at[i], agr.at[i], chip_dev(off))
-    send(nall.at[core, my_rows], nall.at[core, my_rows], fws.at[7], fwr.at[7], partner)
-    for i in reversed(range(len(CHIPS))):
-        rows = pl.ds(pl.multiple_of(back(CHIPS[i]) * 16, 16), 16)
-        arrive(nall.at[core, rows], ags.at[i], agr.at[i])
-        send(nall.at[core, rows], nall.at[core, rows], fws.at[i], fwr.at[i], partner)
-
-    loads["uw"].wait()
-    acc = nn(nall[core], uw[pl.ds(pl.multiple_of(core * HALF, HALF), HALF), :])
-    for i in range(len(CHIPS)):
-        rows = pl.ds(pl.multiple_of(back(CHIPS[i]) * 16, 16), 16)
-        arrive(nall.at[other, rows], fws.at[i], fwr.at[i])
-    arrive(nall.at[other, my_rows], fws.at[7], fwr.at[7])
-    acc = acc + nn(nall[other], uw[pl.ds(pl.multiple_of(other * HALF, HALF), HALF), :])
-    hid = (acc * (0.5 * (1.0 + erf(acc * (0.5**0.5))))).astype(BF16)
-
-    loads["dw"].wait()
+    gain_at = pl.multiple_of(core * HALF, HALF)
+    gain_16 = jnp.concatenate(
+        [
+            jnp.broadcast_to(gain[0:1, pl.ds(gain_at, HALF // 2)], (8, HALF // 2)),
+            jnp.broadcast_to(gain[0:1, pl.ds(gain_at + HALF // 2, HALF // 2)], (8, HALF // 2)),
+        ],
+        axis=0,
+    )
+
+    def both(v):
+        return v[0:8] + v[8:16]
+
+    def twice(v):
+        return jnp.concatenate([v, v], axis=0)
+
+    lane = lax.broadcasted_iota(jnp.int32, (8, 128), 1)
+    for a in range(2):
+        tot = rs_s[a, chip].astype(F32)
+        for i in reversed(range(len(CHIPS))):
+            arrive(rs_r.at[a, i], r1s.at[a, i], r1r.at[a, i])
+            tot = tot + rs_r[a, i].astype(F32)
+        mean_a = both(jnp.sum(tot, axis=1, keepdims=True)) * (1.0 / HALF)
+        cent = tot - twice(mean_a)
+        m2_a = both(jnp.sum(cent * cent, axis=1, keepdims=True))
+        st_s[a] = jnp.where(lane < 64, mean_a, m2_a)
+        send(st_s.at[a], st_r.at[a], sts.at[a], strv.at[a], partner)
+        mixed[a, :, 0 : HALF // 2] = tot[0:8]
+        mixed[a, :, HALF // 2 : HALF] = tot[8:16]
+        arrive(st_r.at[a], sts.at[a], strv.at[a])
+        mean_b, m2_b = st_r[a, :, 0:1], st_r[a, :, 64:65]
+        diff = mean_a - mean_b
+        mean = 0.5 * (mean_a + mean_b)
+        var = (m2_a + m2_b + diff * diff * (HALF / 2)) * (1.0 / D)
+        nall[a, core, chip] = ((tot - twice(mean)) * twice(lax.rsqrt(var + 1e-05)) * gain_16).astype(BF16)
+        mine = nall.at[a, core, chip]
+        for i, off in enumerate(CHIPS):
+            send(mine, mine, ags.at[a, i], agr.at[a, i], chip_dev(off))
+        send(mine, mine, fws.at[a, 7], fwr.at[a, 7], partner)
+
+    def up_half(a, half):
+        blocks = [nall[a, half, k].astype(F32) for k in range(NCHIP)]
+        out = None
+        for part in range(2):
+            lhs = jnp.concatenate([v[8 * part : 8 * part + 8] for v in blocks], axis=0).astype(BF16)
+            at = pl.multiple_of(half * HALF + part * (HALF // 2), HALF // 2)
+            t = nn(lhs, uw[pl.ds(at, HALF // 2), :])
+            out = t if out is None else out + t
+        return out
+
     order = CHIPS + ((0, 0),)
 
-    def unit_term(off, which):
+    def unit_term(hid, a, off, which):
         block = chip_at(off) * 2 + which
-        t = nn(hid, dw[:, pl.ds(pl.multiple_of(block * COLS, COLS), COLS)])
+        tmp[...] = nn(hid, dw[:, pl.ds(pl.multiple_of(block * COLS, COLS), COLS)])
         inner = lax.rem(block, NCHIP)
-        add = mixed[:, pl.ds(pl.multiple_of(inner * COLS, COLS), COLS)]
-        tmp[...] = t
-        tmp[my_rows, :] = tmp[my_rows, :] + jnp.where(block // NCHIP == core, add, 0.0)
+        add = mixed[a, :, pl.ds(pl.multiple_of(inner * COLS, COLS), COLS)]
+        mine = pl.ds(pl.multiple_of(chip * 8, 8), 8)
+        tmp[mine, :] = tmp[mine, :] + jnp.where(block // NCHIP == core, add, 0.0)
         return tmp[...]
 
-    for i, off in enumerate(order):
-        pre2_s[i] = unit_term(off, other).astype(BF16)
-        send(pre2_s.at[i], pre2_r.at[i], p2s.at[i], p2r.at[i], partner)
-    out = None
-    for i, off in enumerate(order):
-        t = unit_term(off, core)
-        arrive(pre2_r.at[i], p2s.at[i], p2r.at[i])
-        t = t + pre2_r[i].astype(F32)
-        if i < len(CHIPS):
-            rs2_s[i] = t.astype(BF16)
-            send(rs2_s.at[i], rs2_r.at[i], r2s.at[i], r2r.at[i], chip_dev(off))
-        else:
-            out = t
-    for i in reversed(range(len(CHIPS))):
-        arrive(rs2_r.at[i], r2s.at[i], r2r.at[i])
-        out = out + rs2_r[i].astype(F32)
-    row_live = lax.broadcasted_iota(jnp.int32, (ROWS, COLS), 0) < my_len
-    lay_out[...] = jnp.where(row_live, out, 0.0).astype(BF16)
+    for a in range(2):
+        for i in reversed(range(len(CHIPS))):
+            src = nall.at[a, core, back(CHIPS[i])]
+            arrive(src, ags.at[a, i], agr.at[a, i])
+            send(src, src, fws.at[a, i], fwr.at[a, i], partner)
+        if a == 0:
+            loads["uw"].wait()
+        acc = up_half(a, core)
+        for i in range(len(CHIPS)):
+            arrive(nall.at[a, other, back(CHIPS[i])], fws.at[a, i], fwr.at[a, i])
+        arrive(nall.at[a, other, chip], fws.at[a, 7], fwr.at[a, 7])
+        acc = acc + up_half(a, other)
+        hid = (acc * (0.5 * (1.0 + erf(acc * (0.5**0.5))))).astype(BF16)
+        if a == 0:
+            loads["dw"].wait()
+        for i, off in enumerate(order):
+            pre2_s[a, i] = unit_term(hid, a, off, other).astype(BF16)
+            send(pre2_s.at[a, i], pre2_r.at[a, i], p2s.at[a, i], p2r.at[a, i], partner)
+        for i, off in enumerate(order):
+            t = unit_term(hid, a, off, core)
+            arrive(pre2_r.at[a, i], p2s.at[a, i], p2r.at[a, i])
+            t = t + pre2_r[a, i].astype(F32)
+            if i < len(CHIPS):
+                rs2_s[a, i] = t.astype(BF16)
+                send(rs2_s.at[a, i], rs2_r.at[a, i], r2s.at[a, i], r2r.at[a, i], chip_dev(off))
+            else:
+                outk[a] = t
+    row_i = lax.broadcasted_iota(jnp.int32, (HR, COLS), 0)
+    for a in range(2):
+        out = outk[a]
+        for i in reversed(range(len(CHIPS))):
+            arrive(rs2_r.at[a, i], r2s.at[a, i], r2r.at[a, i])
+            out = out + rs2_r[a, i].astype(F32)
+        lay_out[rows_of(a), :] = jnp.where(row_i + a * HR < my_len, out, 0.0).astype(BF16)
     for cp in sends:
         cp.wait_send()
 
@@ -481,17 +521,18 @@
             vm((ROWS, 512), F32),
             vm((n, ROWS, 512), BF16),
             vm((n, ROWS, 512), BF16),
-            vm((ROWS, HALF), BF16),
-            vm((nc, 16, HALF), BF16),
-            vm((16, 128), F32),
-            vm((16, 128), F32),
-            vm((16, HALF), F32),
-            vm((2, ROWS, HALF), BF16),
-            vm((ROWS, COLS), F32),
-            vm((8, ROWS, COLS), BF16),
-            vm((8, ROWS, COLS), BF16),
-            vm((nc, ROWS, COLS), BF16),
-            vm((nc, ROWS, COLS), BF16),
+            vm((2, NCHIP, 16, HALF // 2), BF16),
+            vm((2, nc, 16, HALF // 2), BF16),
+            vm((2, 8, 128), F32),
+            vm((2, 8, 128), F32),
+            vm((2, 8, HALF), F32),
+            vm((2, 2, NCHIP, 16, HALF // 2), BF16),
+            vm((HR, COLS), F32),
+            vm((2, HR, COLS), F32),
+            vm((2, 8, HR, COLS), BF16),
+            vm((2, 8, HR, COLS), BF16),
+            vm((2, nc, HR, COLS), BF16),
+            vm((2, nc, HR, COLS), BF16),
             dma((8,)),
             dma((3,)),
             dma((3,)),
@@ -501,18 +542,18 @@
             dma((3,)),
             dma((n,)),
             dma((n,)),
-            dma((nc,)),
-            dma((nc,)),
-            dma((1,)),
-            dma((1,)),
-            dma((nc,)),
-            dma((nc,)),
-            dma((8,)),
-            dma((8,)),
-            dma((8,)),
-            dma((8,)),
-            dma((nc,)),
-            dma((nc,)),
+            dma((2, nc)),
+            dma((2, nc)),
+            dma((2,)),
+            dma((2,)),
+            dma((2, nc)),
+            dma((2, nc)),
+            dma((2, 8)),
+            dma((2, 8)),
+            dma((2, 8)),
+            dma((2, 8)),
+            dma((2, nc)),
+            dma((2, nc)),
         ],
         compiler_params=pltpu.CompilerParams(
             collective_id=0, has_side_effects=True, vmem_limit_bytes=56 * 2**20

time: 77.5 us -> 76.1 us (0.982)
  Pallas kernels: 73.8 us -> 72.3 us
    pallas_call x1, Pallas kernels: 73.8 us -> 72.3 us  [shards(): pl.pallas_call(kernel, out_shape=[jax.ShapeDtypeStruct((ROWS, COLS), BF16...]
where the time goes in v3:
time: 76.1 us; the launch traced here: 75.9 us
  Pallas kernels  72.3 us (95%)
  local copies, waits for them, and re-layouts  2.95 us (4%)
    pallas_call x1, Pallas kernels, shards(): pl.pallas_call(kernel, out_shape=[jax.ShapeDtypeStruct((ROWS, COLS), BF16...  72.3 us
    unnamed x2, local copies, waits for them, and re-layouts  2.95 us

profile of v3, /device:TPU:1, one launch (start us, length us, event | category | flops | bytes accessed | tf_op | source)
XLA Modules:
  0.0 75.9 jit_solution(4993186874632284423)
XLA Ops:
  0.6 72.3 %prefill_layer.1 = (bf16[128,256]{1,0:T(8,128)(2,1)}, bf16[128,256]{1,0:T(8,128)(2,1)}) custom-call(s32[16]{0:T(128)} %len_ref.1, s32[16]{0:T(128)} %grp_ref.1, s32[16]{0:T(128)} %own_ref.1, bf16[128,256]{1,0:T(8,128)(2,1)} %q_hbm.1, bf16[2,128,256]{2,1,0:T(8,128)(2,1)} %skv_hbm.1, bf16[2,512,256]{2,1,0:T(8,128)(2,1)} %pkv_hbm.1, bf16[128,256]{1,0:T(8,128)(2,1)} %res_hbm.1, ...), custom_call_target="tpu_custom_call" | custom-call | tf_op jit(solution)/shard_map/prefill_layer/pallas_call | solution.py:500
  73.0 1.5 %copy.15 = bf16[128,256]{1,0:T(8,128)(2,1)} copy(bf16[128,256]{1,0:T(8,128)(2,1)} %get-tuple-element.4) | data formatting | bytes 131072
  74.4 1.5 %copy.16 = bf16[128,256]{1,0:T(8,128)(2,1)} copy(bf16[128,256]{1,0:T(8,128)(2,1)} %get-tuple-element.5) | data formatting | bytes 131072

commit v4 on v3

--- a/solution.py
+++ b/solution.py
@@ -28,7 +28,8 @@
 UNITS = 512
 HR = ROWS // 2
 STAT = 16
-SLOT = COLS + STAT
+SLOT = DH + STAT
+LOG2E = 1.4426950408889634
 
 Z_FAR = (2, 1, 3)
 CHIPS = ((1, 2), (1, 1), (1, 3), (0, 2), (1, 0), (0, 1), (0, 3))
@@ -45,8 +46,12 @@
     return lax.dot_general(a, b, (((1,), (0,)), ((), ())), preferred_element_type=F32)
 
 
-def slope_of(head):
-    k = head + 1
+def head(h):
+    return slice(h * DH, (h + 1) * DH)
+
+
+def slope_of(index):
+    k = index + 1
     whole, part = k // 4, lax.rem(k, 4)
     out = jnp.float32(1.0)
     for i in range(1, 9):
@@ -64,49 +69,31 @@
     return hi, mid, rest - mid
 
 
-def pack_stats(ms, ls):
+def pack_stats(m, l):
     row = lax.broadcasted_iota(jnp.int32, (STAT, ROWS), 0)
     out = jnp.zeros((STAT, ROWS), F32)
-    at = 0
-    for m, l in zip(ms, ls):
-        for part in split3(m) + split3(l):
-            out = jnp.where(row == at, part, out)
-            at += 1
+    for at, part in enumerate(split3(m) + split3(l)):
+        out = jnp.where(row == at, part, out)
     return out.astype(BF16)
 
 
-def unpack_stats(block):
-    st = block.astype(F32)
-    ms, ls = [], []
-    for h in range(2):
-        at = 6 * h
-        ms.append(st[at : at + 1] + st[at + 1 : at + 2] + st[at + 2 : at + 3])
-        ls.append(st[at + 3 : at + 4] + st[at + 4 : at + 5] + st[at + 5 : at + 6])
-    return ms, ls
-
-
 def combine(parts):
-    ms, ls, os = [], [], []
-    for h in range(2):
-        m = parts[0][0][h]
-        for part in parts[1:]:
-            m = jnp.maximum(m, part[0][h])
-        l, o = None, None
-        for part in parts:
-            scale = jnp.exp(part[0][h] - m)
-            pl_, po = part[1][h] * scale, part[2][h] * scale
-            l = pl_ if l is None else l + pl_
-            o = po if o is None else o + po
-        ms.append(m)
-        ls.append(l)
-        os.append(o)
-    return ms, ls, os
+    m = parts[0][0]
+    for part in parts[1:]:
+        m = jnp.maximum(m, part[0])
+    l, o = None, None
+    for part in parts:
+        scale = jnp.exp2(part[0] - m)
+        l = part[1] * scale if l is None else l + part[1] * scale
+        o = part[2] * scale if o is None else o + part[2] * scale
+    return m, l, o
 
 
 def read_slot(ref, lead):
-    ms, ls = unpack_stats(ref[lead + (pl.ds(COLS, STAT), slice(None))])
-    os = [ref[lead + (pl.ds(h * DH, DH), slice(None))].astype(F32) for h in range(2)]
-    return ms, ls, os
+    st = ref[lead + (pl.ds(DH, STAT), slice(None))].astype(F32)
+    m = st[0:1] + st[1:2] + st[2:3]
+    l = st[3:4] + st[4:5] + st[5:6]
+    return m, l, ref[lead + (pl.ds(0, DH), slice(None))].astype(F32)
 
 
 def erf(x):
@@ -138,6 +125,8 @@
     vt,
     sufo,
     sufs,
+    kbias,
+    sbuf,
     acco,
     accs,
     zsend,
@@ -161,6 +150,7 @@
     qzs,
     qzr,
     kvs,
+    fks,
     kvr,
     pzs,
     pzr,
@@ -222,7 +212,10 @@
         (
             ("q", q_hbm, qz.at[0]),
             ("skv", skv_hbm, skv),
-            ("pkv", pkv_hbm, kvb.at[0]),
+            ("pkv00", pkv_hbm.at[0, :, head(0)], kvb.at[0, 0, 0]),
+            ("pkv10", pkv_hbm.at[1, :, head(0)], kvb.at[0, 1, 0]),
+            ("pkv01", pkv_hbm.at[0, :, head(1)], kvb.at[0, 0, 1]),
+            ("pkv11", pkv_hbm.at[1, :, head(1)], kvb.at[0, 1, 1]),
             ("res", res_hbm, res),
             ("gain", gain_hbm, gain),
             ("ow", ow_hbm, ow),
@@ -243,13 +236,14 @@
     right, left = req_dev(0, 1), req_dev(0, 3)
     for i, d in enumerate(Z_FAR):
         send(q_hbm, qz.at[4 - d], qzs.at[d - 1], qzr.at[3 - d], req_dev(d, 0))
-    send(pkv_hbm.at[0], kvb.at[3, 0], kvs.at[0, 0], kvr.at[3, 0], right)
-    send(pkv_hbm.at[1], kvb.at[1, 1], kvs.at[1, 0], kvr.at[1, 1], left)
-    send(pkv_hbm.at[1], kvb.at[3, 1], kvs.at[0, 1], kvr.at[3, 1], right)
-    send(pkv_hbm.at[0], kvb.at[1, 0], kvs.at[1, 1], kvr.at[1, 0], left)
-
-    def arrive_kv(dx, part):
-        arrive(kvb.at[dx, part], kvs.at[0, 0], kvr.at[dx, part])
+    for h in range(2):
+        for first in range(2):
+            k, v = first, 1 - first
+            send(pkv_hbm.at[k, :, head(h)], kvb.at[3, k, h], kvs.at[0, k, h], kvr.at[3, k, h], right)
+            send(pkv_hbm.at[v, :, head(h)], kvb.at[1, v, h], kvs.at[1, v, h], kvr.at[1, v, h], left)
+
+    def arrive_kv(dx, part, h):
+        arrive(kvb.at[dx, part, h], kvs.at[0, 0, 0], kvr.at[dx, part, h])
 
     my_len = len_ref[me_r]
     slopes = [slope_of(2 * me_m + h) for h in range(2)]
@@ -260,91 +254,98 @@
     slot_i = lax.broadcasted_iota(jnp.int32, (S_MAX, ROWS), 1)
     allowed = (key_i <= slot_i) & (key_i < my_len)
     gap = (slot_i - key_i).astype(F32)
+    pkey = lax.broadcasted_iota(jnp.int32, (KB, ROWS), 0).astype(F32)
     for h in range(2):
-        cols = slice(h * DH, (h + 1) * DH)
-        s = nt(skv[0, :, cols], qz[0, :, cols]) * scale - slopes[h] * gap
+        s = (nt(skv[0, :, head(h)], qz[0, :, head(h)]) * scale - slopes[h] * gap) * LOG2E
         s = jnp.where(allowed, s, NEG)
         m = jnp.max(s, axis=0, keepdims=True)
-        w = jnp.where(allowed, jnp.exp(s - m), 0.0)
+        w = jnp.where(allowed, jnp.exp2(s - m), 0.0)
         sufs[2 * h : 2 * h + 1, :] = m
         sufs[2 * h + 1 : 2 * h + 2, :] = jnp.sum(w, axis=0, keepdims=True)
-        sufo[h] = nn(skv[1, :, cols].T, w.astype(BF16))
-
-    arrive_kv(3, 0)
-    send(kvb.at[3, 0], kvb.at[2, 0], kvs.at[0, 2], kvr.at[2, 0], right)
-    arrive_kv(1, 1)
-    send(kvb.at[1, 1], kvb.at[2, 1], kvs.at[1, 2], kvr.at[2, 1], left)
-
-    pkey = lax.broadcasted_iota(jnp.int32, (KB, ROWS), 0)
-    pslot = lax.broadcasted_iota(jnp.int32, (KB, ROWS), 1)
-    loads["pkv"].wait()
+        sufo[h] = nn(skv[1, :, head(h)].T, w.astype(BF16))
+        kbias[h] = pkey * (slopes[h] * LOG2E)
+
+    for h in range(2):
+        arrive_kv(3, 0, h)
+        send(kvb.at[3, 0, h], kvb.at[2, 0, h], fks.at[0, h], kvr.at[2, 0, h], right)
+        arrive_kv(1, 1, h)
+        send(kvb.at[1, 1, h], kvb.at[2, 1, h], fks.at[1, h], kvr.at[2, 1, h], left)
+
+    pslot = lax.broadcasted_iota(jnp.int32, (1, ROWS), 1)
+    for name in ("pkv00", "pkv01", "pkv10", "pkv11"):
+        loads[name].wait()
     for d in (1, 3, 2):
         arrive(qz.at[d], qzs.at[0], qzr.at[d - 1])
-
-    def block_part(dx, dz):
+    step_keys = 256
+
+    def block_parts(dx, h, order):
         logical = own_ref[req_at(0, dx)]
         group = logical // PER_GROUP
         base = (logical - group * PER_GROUP) * KB
-        valid = grp_ref[req_at(dz, 0)] == group
-        dist = (P_SIZE - base + pslot - pkey).astype(F32)
-        ms, ls, os = [], [], []
-        for h in range(2):
-            cols = slice(h * DH, (h + 1) * DH)
-            s = nt(kvb[dx, 0, :, cols], qz[dz, :, cols]) * scale - slopes[h] * dist
-            m = jnp.max(s, axis=0, keepdims=True)
-            w = jnp.exp(s - m)
-            ms.append(jnp.where(valid, m, NEG))
-            ls.append(jnp.sum(w, axis=0, keepdims=True))
-            os.append(nn(vt[h], w.astype(BF16)))
-        return ms, ls, os
-
-    def held(dz):
-        at = 4 * dz
-        return (
-            [accs[at + 2 * h : at + 2 * h + 1, :] for h in range(2)],
-            [accs[at + 2 * h + 1 : at + 2 * h + 2, :] for h in range(2)],
-            [acco[dz, h] for h in range(2)],
-        )
-
-    def hold(dz, part):
-        at = 4 * dz
-        for h in range(2):
-            accs[at + 2 * h : at + 2 * h + 1, :] = part[0][h]
-            accs[at + 2 * h + 1 : at + 2 * h + 2, :] = part[1][h]
-            acco[dz, h] = part[2][h]
-
-    for dx in (0, 1, 3, 2):
+        far = (P_SIZE - base + pslot).astype(F32) * (slopes[h] * LOG2E)
+        tops = []
+        for dz in order:
+            m8 = None
+            for c in range(KB // step_keys):
+                keys = slice(c * step_keys, (c + 1) * step_keys)
+                s = nt(kvb[dx, 0, h, keys, :], qz[dz, :, head(h)]) * (scale * LOG2E) + kbias[h, keys, :]
+                sbuf[dz, keys, :] = s
+                top = jnp.max(s.reshape(step_keys // 8, 8, ROWS), axis=0)
+                m8 = top if m8 is None else jnp.maximum(m8, top)
+            tops.append(jnp.max(m8, axis=0, keepdims=True))
+        out = []
+        for dz, m in zip(order, tops):
+            l8, o = None, None
+            for c in range(KB // step_keys):
+                keys = slice(c * step_keys, (c + 1) * step_keys)
+                w = jnp.exp2(sbuf[dz, keys, :] - m)
+                low = jnp.sum(w.reshape(step_keys // 8, 8, ROWS), axis=0)
+                t = nn(vt[:, keys], w.astype(BF16))
+                l8, o = (low, t) if c == 0 else (l8 + low, o + t)
+            valid = grp_ref[req_at(dz, 0)] == group
+            out.append((jnp.where(valid, m - far, NEG), jnp.sum(l8, axis=0, keepdims=True), o))
+        return out
+
+    def held(dz, h):
+        at = 4 * dz + 2 * h
+        return accs[at : at + 1, :], accs[at + 1 : at + 2, :], acco[dz, h]
+
+    def hold(dz, h, part):
+        at = 4 * dz + 2 * h
+        accs[at : at + 1, :] = part[0]
+        accs[at + 1 : at + 2, :] = part[1]
+        acco[dz, h] = part[2]
+
+    for dx, h in ((0, 0), (0, 1), (1, 0), (3, 0), (1, 1), (3, 1), (2, 0), (2, 1)):
         if dx == 1:
-            arrive_kv(1, 0)
+            arrive_kv(1, 0, h)
         if dx == 3:
-            arrive_kv(3, 1)
+            arrive_kv(3, 1, h)
         if dx == 2:
-            arrive_kv(2, 0)
-            arrive_kv(2, 1)
-        for h in range(2):
-            vt[h] = kvb[dx, 1, :, h * DH : (h + 1) * DH].T
-        for dz in (2, 1, 3, 0):
-            part = block_part(dx, dz)
+            arrive_kv(2, 0, h)
+            arrive_kv(2, 1, h)
+        vt[...] = kvb[dx, 1, h].T
+        rows = (2, 1, 3, 0)
+        for dz, part in zip(rows, block_parts(dx, h, rows)):
             if dx != 0:
-                part = combine([held(dz), part])
+                part = combine([held(dz, h), part])
             if dx != 2 or dz == 0:
-                hold(dz, part)
+                hold(dz, h, part)
             else:
-                ms, ls, os = part
-                for h in range(2):
-                    zsend[dz - 1, h * DH : (h + 1) * DH, :] = os[h].astype(BF16)
-                zsend[dz - 1, COLS:SLOT, :] = pack_stats(ms, ls)
-                send(zsend.at[dz - 1], zrecv.at[dz - 1], pzs.at[dz - 1], pzr.at[dz - 1], req_dev(dz, 0))
-
-    suffix = ([sufs[0:1, :], sufs[2:3, :]], [sufs[1:2, :], sufs[3:4, :]], [sufo[0], sufo[1]])
-    parts = [held(0), suffix]
-    for dz in (1, 3, 2):
-        arrive(zrecv.at[dz - 1], pzs.at[dz - 1], pzr.at[dz - 1])
-        parts.append(read_slot(zrecv, (dz - 1,)))
-    ms, ls, os = combine(parts)
+                zsend[dz - 1, h, 0:DH, :] = part[2].astype(BF16)
+                zsend[dz - 1, h, DH:SLOT, :] = pack_stats(part[0], part[1])
+                send(
+                    zsend.at[dz - 1, h], zrecv.at[dz - 1, h], pzs.at[dz - 1, h], pzr.at[dz - 1, h], req_dev(dz, 0)
+                )
+
     live = lax.broadcasted_iota(jnp.int32, (DH, ROWS), 1) < my_len
     for h in range(2):
-        att_out[:, h * DH : (h + 1) * DH] = jnp.where(live, os[h] / ls[h], 0.0).T.astype(BF16)
+        parts = [held(0, h), (sufs[2 * h : 2 * h + 1, :], sufs[2 * h + 1 : 2 * h + 2, :], sufo[h])]
+        for dz in (1, 3, 2):
+            arrive(zrecv.at[dz - 1, h], pzs.at[dz - 1, h], pzr.at[dz - 1, h])
+            parts.append(read_slot(zrecv, (dz - 1, h)))
+        m, l, o = combine(parts)
+        att_out[:, head(h)] = jnp.where(live, o / l, 0.0).T.astype(BF16)
 
     loads["res"].wait()
     loads["ow"].wait()
@@ -505,19 +506,21 @@
         scratch_shapes=[
             vm((NZH, ROWS, COLS), BF16),
             vm((2, S_MAX, COLS), BF16),
-            vm((NX, 2, KB, COLS), BF16),
+            vm((NX, 2, 2, KB, DH), BF16),
             vm((ROWS, COLS), BF16),
             vm((1, D), F32),
             vm((COLS, D), BF16),
             vm((D, UNITS), BF16),
             vm((UNITS, D), BF16),
-            vm((2, DH, KB), BF16),
+            vm((DH, KB), BF16),
             vm((2, DH, ROWS), F32),
             vm((8, ROWS), F32),
+            vm((2, KB, ROWS), F32),
+            vm((NZH, KB, ROWS), F32),
             vm((NZH, 2, DH, ROWS), F32),
             vm((16, ROWS), F32),
-            vm((3, SLOT, ROWS), BF16),
-            vm((3, SLOT, ROWS), BF16),
+            vm((3, 2, SLOT, ROWS), BF16),
+            vm((3, 2, SLOT, ROWS), BF16),
             vm((ROWS, 512), F32),
             vm((n, ROWS, 512), BF16),
             vm((n, ROWS, 512), BF16),
@@ -533,13 +536,14 @@
             vm((2, 8, HR, COLS), BF16),
             vm((2, nc, HR, COLS), BF16),
             vm((2, nc, HR, COLS), BF16),
-            dma((8,)),
+            dma((11,)),
             dma((3,)),
             dma((3,)),
-            dma((2, 3)),
-            dma((NX, 2)),
-            dma((3,)),
-            dma((3,)),
+            dma((2, 2, 2)),
+            dma((2, 2)),
+            dma((NX, 2, 2)),
+            dma((3, 2)),
+            dma((3, 2)),
             dma((n,)),
             dma((n,)),
             dma((2, nc)),

time: 76.1 us -> 72.7 us (0.955)
  Pallas kernels: 72.3 us -> 68.9 us
    pallas_call x1, Pallas kernels: 72.3 us -> 68.9 us  [shards(): pl.pallas_call(kernel, out_shape=[jax.ShapeDtypeStruct((ROWS, COLS), BF16...]
where the time goes in v4:
time: 72.7 us; the launch traced here: 72.5 us
  Pallas kernels  68.9 us (95%)
  local copies, waits for them, and re-layouts  2.95 us (4%)
    pallas_call x1, Pallas kernels, shards(): pl.pallas_call(kernel, out_shape=[jax.ShapeDtypeStruct((ROWS, COLS), BF16...  68.9 us
    unnamed x2, local copies, waits for them, and re-layouts  2.95 us

profile of v4, /device:TPU:1, one launch (start us, length us, event | category | flops | bytes accessed | tf_op | source)
XLA Modules:
  0.0 72.5 jit_solution(10947110191866389261)
XLA Ops:
  0.6 68.9 %prefill_layer.1 = (bf16[128,256]{1,0:T(8,128)(2,1)}, bf16[128,256]{1,0:T(8,128)(2,1)}) custom-call(s32[16]{0:T(128)} %len_ref.1, s32[16]{0:T(128)} %grp_ref.1, s32[16]{0:T(128)} %own_ref.1, bf16[128,256]{1,0:T(8,128)(2,1)} %q_hbm.1, bf16[2,128,256]{2,1,0:T(8,128)(2,1)} %skv_hbm.1, bf16[2,512,256]{2,1,0:T(8,128)(2,1)} %pkv_hbm.1, bf16[128,256]{1,0:T(8,128)(2,1)} %res_hbm.1, ...), custom_call_target="tpu_custom_call" | custom-call | tf_op jit(solution)/shard_map/prefill_layer/pallas_call | solution.py:501
  69.5 1.5 %copy.15 = bf16[128,256]{1,0:T(8,128)(2,1)} copy(bf16[128,256]{1,0:T(8,128)(2,1)} %get-tuple-element.4) | data formatting | bytes 131072
  71.0 1.5 %copy.16 = bf16[128,256]{1,0:T(8,128)(2,1)} copy(bf16[128,256]{1,0:T(8,128)(2,1)} %get-tuple-element.5) | data formatting | bytes 131072

commit v5 on v4

--- a/solution.py
+++ b/solution.py
@@ -26,6 +26,7 @@
 D = 4096
 HALF = D // 2
 UNITS = 512
+WIDE = 512
 HR = ROWS // 2
 STAT = 16
 SLOT = DH + STAT
@@ -140,8 +141,8 @@
     st_r,
     mixed,
     nall,
-    tmp,
     outk,
+    kept,
     pre2_s,
     pre2_r,
     rs2_s,
@@ -202,6 +203,10 @@
         cp.start()
         sends.append(cp)
 
+    def flush(count):
+        for _ in range(count):
+            sends.pop(0).wait_send()
+
     def arrive(dst, ssem, rsem):
         pltpu.make_async_remote_copy(
             src_ref=dst, dst_ref=dst, send_sem=ssem, recv_sem=rsem, device_id=partner, device_id_type=MESH
@@ -218,9 +223,9 @@
             ("pkv11", pkv_hbm.at[1, :, head(1)], kvb.at[0, 1, 1]),
             ("res", res_hbm, res),
             ("gain", gain_hbm, gain),
-            ("ow", ow_hbm, ow),
+            *((f"ow{n}", ow_hbm.at[:, n * WIDE : (n + 1) * WIDE], ow.at[n]) for n in range(D // WIDE)),
             ("uw", uw_hbm, uw),
-            ("dw", dw_hbm, dw),
+            *((f"dw{n}", dw_hbm.at[:, n * COLS : (n + 1) * COLS], dw.at[n]) for n in range(D // COLS)),
         )
     ):
         loads[name] = pltpu.make_async_copy(src, dst, loc.at[i])
@@ -338,6 +343,11 @@
                     zsend.at[dz - 1, h], zrecv.at[dz - 1, h], pzs.at[dz - 1, h], pzr.at[dz - 1, h], req_dev(dz, 0)
                 )
 
+    for name in loads:
+        if name[:2] in ("ow", "uw", "dw", "re", "ga"):
+            loads[name].wait()
+    flush(len(sends) - 6)
+
     live = lax.broadcasted_iota(jnp.int32, (DH, ROWS), 1) < my_len
     for h in range(2):
         parts = [held(0, h), (sufs[2 * h : 2 * h + 1, :], sufs[2 * h + 1 : 2 * h + 2, :], sufo[h])]
@@ -347,16 +357,13 @@
         m, l, o = combine(parts)
         att_out[:, head(h)] = jnp.where(live, o / l, 0.0).T.astype(BF16)
 
-    loads["res"].wait()
-    loads["ow"].wait()
     respad[...] = jnp.zeros_like(respad)
     respad[:, pl.ds(pl.multiple_of(core * COLS, COLS), COLS)] = res[...].astype(F32)
-    wide = 512
+    wide = WIDE
 
     def head_term(half, n, rows):
-        at = pl.multiple_of(half * HALF + n * wide, wide)
-        t = nn(att_out[rows, :], ow[:, pl.ds(at, wide)])
-        return t + jnp.where(half * (HALF // wide) + n == chip, respad[rows, :], 0.0)
+        block = half * (HALF // wide) + n
+        return nn(att_out[rows, :], ow[block]) + jnp.where(block == chip, respad[rows, :], 0.0)
 
     def rows_of(a):
         return slice(a * HR, (a + 1) * HR)
@@ -379,7 +386,6 @@
                 ).astype(BF16)
         for i, off in enumerate(CHIPS):
             send(rs_s.at[a, chip_at(off)], rs_r.at[a, i], r1s.at[a, i], r1r.at[a, i], chip_dev(off))
-    loads["gain"].wait()
     gain_at = pl.multiple_of(core * HALF, HALF)
     gain_16 = jnp.concatenate(
         [
@@ -431,51 +437,56 @@
 
     order = CHIPS + ((0, 0),)
 
+    my_block = lax.broadcasted_iota(jnp.int32, (HR, COLS), 0) // 8 == chip
+
     def unit_term(hid, a, off, which):
         block = chip_at(off) * 2 + which
-        tmp[...] = nn(hid, dw[:, pl.ds(pl.multiple_of(block * COLS, COLS), COLS)])
         inner = lax.rem(block, NCHIP)
         add = mixed[a, :, pl.ds(pl.multiple_of(inner * COLS, COLS), COLS)]
-        mine = pl.ds(pl.multiple_of(chip * 8, 8), 8)
-        tmp[mine, :] = tmp[mine, :] + jnp.where(block // NCHIP == core, add, 0.0)
-        return tmp[...]
+        add = jnp.where(block // NCHIP == core, add, 0.0)
+        return nn(hid, dw[block]) + jnp.where(my_block, jnp.concatenate([add] * (HR // 8), axis=0), 0.0)
 
     for a in range(2):
         for i in reversed(range(len(CHIPS))):
             src = nall.at[a, core, back(CHIPS[i])]
             arrive(src, ags.at[a, i], agr.at[a, i])
             send(src, src, fws.at[a, i], fwr.at[a, i], partner)
-        if a == 0:
-            loads["uw"].wait()
         acc = up_half(a, core)
         for i in range(len(CHIPS)):
             arrive(nall.at[a, other, back(CHIPS[i])], fws.at[a, i], fwr.at[a, i])
         arrive(nall.at[a, other, chip], fws.at[a, 7], fwr.at[a, 7])
         acc = acc + up_half(a, other)
         hid = (acc * (0.5 * (1.0 + erf(acc * (0.5**0.5))))).astype(BF16)
-        if a == 0:
-            loads["dw"].wait()
+        for g in (0, 4):
+            for i in range(g, g + 4):
+                pre2_s[a, i] = unit_term(hid, a, order[i], other).astype(BF16)
+            for i in range(g, g + 4):
+                send(pre2_s.at[a, i], pre2_r.at[a, i], p2s.at[a, i], p2r.at[a, i], partner)
         for i, off in enumerate(order):
-            pre2_s[a, i] = unit_term(hid, a, off, other).astype(BF16)
-            send(pre2_s.at[a, i], pre2_r.at[a, i], p2s.at[a, i], p2r.at[a, i], partner)
+            outk[i] = unit_term(hid, a, off, core)
         for i, off in enumerate(order):
-            t = unit_term(hid, a, off, core)
             arrive(pre2_r.at[a, i], p2s.at[a, i], p2r.at[a, i])
-            t = t + pre2_r[a, i].astype(F32)
+            t = outk[i] + pre2_r[a, i].astype(F32)
             if i < len(CHIPS):
                 rs2_s[a, i] = t.astype(BF16)
                 send(rs2_s.at[a, i], rs2_r.at[a, i], r2s.at[a, i], r2r.at[a, i], chip_dev(off))
             else:
-                outk[a] = t
+                kept[a] = t
+    flush(len(sends) - len(CHIPS))
     row_i = lax.broadcasted_iota(jnp.int32, (HR, COLS), 0)
     for a in range(2):
-        out = outk[a]
+        out = kept[a]
         for i in reversed(range(len(CHIPS))):
             arrive(rs2_r.at[a, i], r2s.at[a, i], r2r.at[a, i])
             out = out + rs2_r[a, i].astype(F32)
         lay_out[rows_of(a), :] = jnp.where(row_i + a * HR < my_len, out, 0.0).astype(BF16)
     for cp in sends:
         cp.wait_send()
+
+
+def hand_over(att_ref, lay_ref, att_out, lay_out):
+    att_out[...] = att_ref[...]
+    lay_out[...] = lay_ref[...]
 
 
 def shards(
@@ -498,7 +509,7 @@
     vm = pltpu.VMEM
     n = HALF // 512
     nc = len(CHIPS)
-    return pl.pallas_call(
+    results = pl.pallas_call(
         kernel,
         out_shape=[jax.ShapeDtypeStruct((ROWS, COLS), BF16)] * 2,
         in_specs=[smem] * 3 + [anym] * 8,
@@ -509,9 +520,9 @@
             vm((NX, 2, 2, KB, DH), BF16),
             vm((ROWS, COLS), BF16),
             vm((1, D), F32),
-            vm((COLS, D), BF16),
+            vm((D // WIDE, COLS, WIDE), BF16),
             vm((D, UNITS), BF16),
-            vm((UNITS, D), BF16),
+            vm((D // COLS, UNITS, COLS), BF16),
             vm((DH, KB), BF16),
             vm((2, DH, ROWS), F32),
             vm((8, ROWS), F32),
@@ -530,13 +541,13 @@
             vm((2, 8, 128), F32),
             vm((2, 8, HALF), F32),
             vm((2, 2, NCHIP, 16, HALF // 2), BF16),
-            vm((HR, COLS), F32),
+            vm((8, HR, COLS), F32),
             vm((2, HR, COLS), F32),
             vm((2, 8, HR, COLS), BF16),
             vm((2, 8, HR, COLS), BF16),
             vm((2, nc, HR, COLS), BF16),
             vm((2, nc, HR, COLS), BF16),
-            dma((11,)),
+            dma((40,)),
             dma((3,)),
             dma((3,)),
             dma((2, 2, 2)),
@@ -576,6 +587,13 @@
         up_weight,
         down_weight,
     )
+    return pl.pallas_call(
+        hand_over,
+        out_shape=[jax.ShapeDtypeStruct((ROWS, COLS), BF16)] * 2,
+        in_specs=[vmem] * 2,
+        out_specs=[vmem] * 2,
+        name="hand_over",
+    )(*results)
 
 
 def solution(mesh):

time: 72.7 us -> 68.2 us (0.938)
  local copies, waits for them, and re-layouts: 2.95 us -> 0 us
  Pallas kernels: 68.9 us -> 67.4 us
    pallas_call x1, Pallas kernels: 68.9 us -> 65.9 us  [shards(): pl.pallas_call(kernel, out_shape=[jax.ShapeDtypeStruct((ROWS, COLS), BF16...]
    unnamed x2 -> x0, local copies, waits for them, and re-layouts: 2.95 us -> none
    pallas_call x0 -> x1, Pallas kernels: none -> 1.53 us  [shards(): pl.pallas_call(hand_over, out_shape=[jax.ShapeDtypeStruct((ROWS, COLS), B...]
where the time goes in v5:
time: 68.2 us; the launch traced here: 68.1 us
  Pallas kernels  67.4 us (99%)
    pallas_call x1, Pallas kernels, shards(): pl.pallas_call(kernel, out_shape=[jax.ShapeDtypeStruct((ROWS, COLS), BF16...  65.9 us
    pallas_call x1, Pallas kernels, shards(): pl.pallas_call(hand_over, out_shape=[jax.ShapeDtypeStruct((ROWS, COLS), B...  1.53 us

profile of v5, /device:TPU:1, one launch (start us, length us, event | category | flops | bytes accessed | tf_op | source)
XLA Modules:
  0.0 68.1 jit_solution(3122208959980482430)
XLA Ops:
  0.6 65.9 %prefill_layer.1 = (bf16[128,256]{1,0:T(8,128)(2,1)}, bf16[128,256]{1,0:T(8,128)(2,1)}) custom-call(s32[16]{0:T(128)} %len_ref.1, s32[16]{0:T(128)} %grp_ref.1, s32[16]{0:T(128)} %own_ref.1, bf16[128,256]{1,0:T(8,128)(2,1)} %q_hbm.1, bf16[2,128,256]{2,1,0:T(8,128)(2,1)} %skv_hbm.1, bf16[2,512,256]{2,1,0:T(8,128)(2,1)} %pkv_hbm.1, bf16[128,256]{1,0:T(8,128)(2,1)} %res_hbm.1, ...), custom_call_target="tpu_custom_call" | custom-call | tf_op jit(solution)/shard_map/prefill_layer/pallas_call | solution.py:512
  66.6 1.5 %hand_over.1 = (bf16[128,256]{1,0:T(8,128)(2,1)}, bf16[128,256]{1,0:T(8,128)(2,1)}) custom-call(bf16[128,256]{1,0:T(8,128)(2,1)} %get-tuple-element.4.att_ref, bf16[128,256]{1,0:T(8,128)(2,1)} %get-tuple-element.5.lay_ref), custom_call_target="tpu_custom_call" | custom-call | tf_op jit(solution)/shard_map/hand_over/pallas_call | solution.py:590

commit v6 on v5

--- a/solution.py
+++ b/solution.py
@@ -32,7 +32,6 @@
 SLOT = DH + STAT
 LOG2E = 1.4426950408889634
 
-Z_FAR = (2, 1, 3)
 CHIPS = ((1, 2), (1, 1), (1, 3), (0, 2), (1, 0), (0, 1), (0, 3))
 
 F32 = jnp.float32
@@ -148,6 +147,9 @@
     rs2_s,
     rs2_r,
     loc,
+    seen_z,
+    seen_mp,
+    seen_far,
     qzs,
     qzr,
     kvs,
@@ -194,67 +196,84 @@
         return (me_r, chip_at(off) * 2 + core)
 
     partner = (me_r, chip * 2 + other)
-    sends = []
 
     def send(src, dst, ssem, rsem, dev):
-        cp = pltpu.make_async_remote_copy(
+        pltpu.make_async_remote_copy(
             src_ref=src, dst_ref=dst, send_sem=ssem, recv_sem=rsem, device_id=dev, device_id_type=MESH
+        ).start()
+
+    def both_ends(ref, ssem, rsem):
+        return pltpu.make_async_remote_copy(
+            src_ref=ref, dst_ref=ref, send_sem=ssem, recv_sem=rsem, device_id=partner, device_id_type=MESH
         )
-        cp.start()
-        sends.append(cp)
-
-    def flush(count):
-        for _ in range(count):
-            sends.pop(0).wait_send()
-
-    def arrive(dst, ssem, rsem):
-        pltpu.make_async_remote_copy(
-            src_ref=dst, dst_ref=dst, send_sem=ssem, recv_sem=rsem, device_id=partner, device_id_type=MESH
-        ).wait_recv()
-
-    loads = {}
-    for i, (name, src, dst) in enumerate(
-        (
-            ("q", q_hbm, qz.at[0]),
-            ("skv", skv_hbm, skv),
-            ("pkv00", pkv_hbm.at[0, :, head(0)], kvb.at[0, 0, 0]),
-            ("pkv10", pkv_hbm.at[1, :, head(0)], kvb.at[0, 1, 0]),
-            ("pkv01", pkv_hbm.at[0, :, head(1)], kvb.at[0, 0, 1]),
-            ("pkv11", pkv_hbm.at[1, :, head(1)], kvb.at[0, 1, 1]),
-            ("res", res_hbm, res),
-            ("gain", gain_hbm, gain),
-            *((f"ow{n}", ow_hbm.at[:, n * WIDE : (n + 1) * WIDE], ow.at[n]) for n in range(D // WIDE)),
-            ("uw", uw_hbm, uw),
-            *((f"dw{n}", dw_hbm.at[:, n * COLS : (n + 1) * COLS], dw.at[n]) for n in range(D // COLS)),
-        )
-    ):
-        loads[name] = pltpu.make_async_copy(src, dst, loc.at[i])
-        loads[name].start()
+
+    def arrive(ref, rsem):
+        both_ends(ref, rsem, rsem).wait_recv()
+
+    def sent(ref, ssem):
+        both_ends(ref, ssem, ssem).wait_send()
 
     barrier = pltpu.get_barrier_semaphore()
-    peers = [req_dev(d, 0) for d in Z_FAR] + [req_dev(0, d) for d in (1, 3)]
-    peers += [chip_dev(o) for o in CHIPS] + [partner]
-    for dev in peers:
+    z_near = [req_dev(1, 0), req_dev(3, 0)]
+    mp_near = [chip_dev((0, 1)), chip_dev((0, 3)), chip_dev((1, 0))]
+    near = [req_dev(0, 1), req_dev(0, 3)] + z_near + mp_near + [partner]
+    for dev in near:
         pl.semaphore_signal(barrier, inc=1, device_id=dev, device_id_type=MESH)
-    pl.semaphore_wait(barrier, len(peers))
+
+    loads = {
+        "q": qz.at[0],
+        "skv": skv,
+        "pkv": kvb.at[0],
+        "res": res,
+        "gain": gain,
+        "ow": ow,
+        "uw": uw,
+        "dw": dw,
+    }
+    pieces = [("q", q_hbm, qz.at[0]), ("skv", skv_hbm, skv)]
+    pieces += [("pkv", pkv_hbm.at[p, :, head(h)], kvb.at[0, p, h]) for h in range(2) for p in range(2)]
+    pieces += [("res", res_hbm, res), ("gain", gain_hbm, gain)]
+    pieces += [("ow", ow_hbm.at[:, n * WIDE : (n + 1) * WIDE], ow.at[n]) for n in range(D // WIDE)]
+    pieces += [("uw", uw_hbm, uw)]
+    pieces += [("dw", dw_hbm.at[:, n * COLS : (n + 1) * COLS], dw.at[n]) for n in range(D // COLS)]
+    names = list(loads)
+
+    def load(wanted):
+        for name, src, dst in pieces:
+            if name in wanted:
+                pltpu.make_async_copy(src, dst, loc.at[names.index(name)]).start()
+
+    def loaded(name):
+        pltpu.make_async_copy(loads[name], loads[name], loc.at[names.index(name)]).wait()
+
+    load(("q", "skv", "pkv"))
+    pl.semaphore_wait(barrier, len(near))
 
     right, left = req_dev(0, 1), req_dev(0, 3)
-    for i, d in enumerate(Z_FAR):
-        send(q_hbm, qz.at[4 - d], qzs.at[d - 1], qzr.at[3 - d], req_dev(d, 0))
+    for dev in z_near:
+        pl.semaphore_signal(seen_z, inc=1, device_id=dev, device_id_type=MESH)
+    for dev in mp_near:
+        pl.semaphore_signal(seen_mp, inc=1, device_id=dev, device_id_type=MESH)
     for h in range(2):
         for first in range(2):
             k, v = first, 1 - first
-            send(pkv_hbm.at[k, :, head(h)], kvb.at[3, k, h], kvs.at[0, k, h], kvr.at[3, k, h], right)
-            send(pkv_hbm.at[v, :, head(h)], kvb.at[1, v, h], kvs.at[1, v, h], kvr.at[1, v, h], left)
+            send(pkv_hbm.at[k, :, head(h)], kvb.at[3, k, h], kvs, kvr.at[2, k, h], right)
+            send(pkv_hbm.at[v, :, head(h)], kvb.at[1, v, h], kvs, kvr.at[0, v, h], left)
+        if h == 0:
+            for d in (1, 3):
+                send(q_hbm, qz.at[4 - d], qzs, qzr, req_dev(d, 0))
+    pl.semaphore_wait(seen_z, 2)
+    send(q_hbm, qz.at[2], qzs, qzr, req_dev(2, 0))
+    load(("res", "gain", "ow", "uw", "dw"))
 
     def arrive_kv(dx, part, h):
-        arrive(kvb.at[dx, part, h], kvs.at[0, 0, 0], kvr.at[dx, part, h])
+        arrive(kvb.at[dx, part, h], kvr.at[dx - 1, part, h])
 
     my_len = len_ref[me_r]
     slopes = [slope_of(2 * me_m + h) for h in range(2)]
     scale = float(DH) ** (-0.5)
-    loads["q"].wait()
-    loads["skv"].wait()
+    loaded("q")
+    loaded("skv")
     key_i = lax.broadcasted_iota(jnp.int32, (S_MAX, ROWS), 0)
     slot_i = lax.broadcasted_iota(jnp.int32, (S_MAX, ROWS), 1)
     allowed = (key_i <= slot_i) & (key_i < my_len)
@@ -272,15 +291,13 @@
 
     for h in range(2):
         arrive_kv(3, 0, h)
-        send(kvb.at[3, 0, h], kvb.at[2, 0, h], fks.at[0, h], kvr.at[2, 0, h], right)
+        send(kvb.at[3, 0, h], kvb.at[2, 0, h], fks, kvr.at[1, 0, h], right)
         arrive_kv(1, 1, h)
-        send(kvb.at[1, 1, h], kvb.at[2, 1, h], fks.at[1, h], kvr.at[2, 1, h], left)
+        send(kvb.at[1, 1, h], kvb.at[2, 1, h], fks, kvr.at[1, 1, h], left)
 
     pslot = lax.broadcasted_iota(jnp.int32, (1, ROWS), 1)
-    for name in ("pkv00", "pkv01", "pkv10", "pkv11"):
-        loads[name].wait()
-    for d in (1, 3, 2):
-        arrive(qz.at[d], qzs.at[0], qzr.at[d - 1])
+    loaded("pkv")
+    arrive(qz.at[pl.ds(1, 3)], qzr)
     step_keys = 256
 
     def block_parts(dx, h, order):
@@ -337,23 +354,25 @@
             if dx != 2 or dz == 0:
                 hold(dz, h, part)
             else:
-                zsend[dz - 1, h, 0:DH, :] = part[2].astype(BF16)
-                zsend[dz - 1, h, DH:SLOT, :] = pack_stats(part[0], part[1])
-                send(
-                    zsend.at[dz - 1, h], zrecv.at[dz - 1, h], pzs.at[dz - 1, h], pzr.at[dz - 1, h], req_dev(dz, 0)
-                )
-
-    for name in loads:
-        if name[:2] in ("ow", "uw", "dw", "re", "ga"):
-            loads[name].wait()
-    flush(len(sends) - 6)
+                zsend[h, dz - 1, 0:DH, :] = part[2].astype(BF16)
+                zsend[h, dz - 1, DH:SLOT, :] = pack_stats(part[0], part[1])
+                send(zsend.at[h, dz - 1], zrecv.at[h, dz - 1], pzs, pzr.at[h], req_dev(dz, 0))
+
+    for name in ("res", "gain", "ow", "uw", "dw"):
+        loaded(name)
+    sent(qz.at[pl.ds(1, 3)], qzs)
+    sent(kvb.at[pl.ds(0, 2)], kvs)
+    sent(kvb.at[0], fks)
+    pl.semaphore_wait(seen_mp, len(mp_near))
+    pl.semaphore_signal(seen_far, inc=1, device_id=chip_dev((1, 0)), device_id_type=MESH)
+    pl.semaphore_wait(seen_far, 1)
 
     live = lax.broadcasted_iota(jnp.int32, (DH, ROWS), 1) < my_len
     for h in range(2):
         parts = [held(0, h), (sufs[2 * h : 2 * h + 1, :], sufs[2 * h + 1 : 2 * h + 2, :], sufo[h])]
+        arrive(zrecv.at[h], pzr.at[h])
         for dz in (1, 3, 2):
-            arrive(zrecv.at[dz - 1, h], pzs.at[dz - 1, h], pzr.at[dz - 1, h])
-            parts.append(read_slot(zrecv, (dz - 1, h)))
+            parts.append(read_slot(zrecv, (h, dz - 1)))
         m, l, o = combine(parts)
         att_out[:, head(h)] = jnp.where(live, o / l, 0.0).T.astype(BF16)
 
@@ -370,7 +389,7 @@
 
     for n in (0, 2, 1, 3):
         pre_s[n] = head_term(other, n, slice(None)).astype(BF16)
-        send(pre_s.at[n], pre_r.at[n], p1s.at[n], p1r.at[n], partner)
+        send(pre_s.at[n], pre_r.at[n], p1s, p1r.at[n], partner)
 
     for a in range(2):
         for n in range(2):
@@ -378,14 +397,14 @@
             for cn in (n, n + 2):
                 t = head_term(core, cn, rows_of(a))
                 if a == 0:
-                    arrive(pre_r.at[cn], p1s.at[cn], p1r.at[cn])
+                    arrive(pre_r.at[cn], p1r.at[cn])
                 terms.append(t + pre_r[cn, rows_of(a), :].astype(F32))
             for k in range(NCHIP):
                 rs_s[a, k, :, n * wide : (n + 1) * wide] = jnp.concatenate(
                     [t[8 * k : 8 * k + 8] for t in terms], axis=0
                 ).astype(BF16)
         for i, off in enumerate(CHIPS):
-            send(rs_s.at[a, chip_at(off)], rs_r.at[a, i], r1s.at[a, i], r1r.at[a, i], chip_dev(off))
+            send(rs_s.at[a, chip_at(off)], rs_r.at[a, i], r1s, r1r.at[a], chip_dev(off))
     gain_at = pl.multiple_of(core * HALF, HALF)
     gain_16 = jnp.concatenate(
         [
@@ -404,17 +423,17 @@
     lane = lax.broadcasted_iota(jnp.int32, (8, 128), 1)
     for a in range(2):
         tot = rs_s[a, chip].astype(F32)
-        for i in reversed(range(len(CHIPS))):
-            arrive(rs_r.at[a, i], r1s.at[a, i], r1r.at[a, i])
+        arrive(rs_r.at[a], r1r.at[a])
+        for i in range(len(CHIPS)):
             tot = tot + rs_r[a, i].astype(F32)
         mean_a = both(jnp.sum(tot, axis=1, keepdims=True)) * (1.0 / HALF)
         cent = tot - twice(mean_a)
         m2_a = both(jnp.sum(cent * cent, axis=1, keepdims=True))
         st_s[a] = jnp.where(lane < 64, mean_a, m2_a)
-        send(st_s.at[a], st_r.at[a], sts.at[a], strv.at[a], partner)
+        send(st_s.at[a], st_r.at[a], sts, strv.at[a], partner)
         mixed[a, :, 0 : HALF // 2] = tot[0:8]
         mixed[a, :, HALF // 2 : HALF] = tot[8:16]
-        arrive(st_r.at[a], sts.at[a], strv.at[a])
+        arrive(st_r.at[a], strv.at[a])
         mean_b, m2_b = st_r[a, :, 0:1], st_r[a, :, 64:65]
         diff = mean_a - mean_b
         mean = 0.5 * (mean_a + mean_b)
@@ -422,8 +441,8 @@
         nall[a, core, chip] = ((tot - twice(mean)) * twice(lax.rsqrt(var + 1e-05)) * gain_16).astype(BF16)
         mine = nall.at[a, core, chip]
         for i, off in enumerate(CHIPS):
-            send(mine, mine, ags.at[a, i], agr.at[a, i], chip_dev(off))
-        send(mine, mine, fws.at[a, 7], fwr.at[a, 7], partner)
+            send(mine, mine, ags, agr.at[a, i], chip_dev(off))
+        send(mine, mine, fws, fwr.at[a], partner)
 
     def up_half(a, half):
         blocks = [nall[a, half, k].astype(F32) for k in range(NCHIP)]
@@ -449,39 +468,43 @@
     for a in range(2):
         for i in reversed(range(len(CHIPS))):
             src = nall.at[a, core, back(CHIPS[i])]
-            arrive(src, ags.at[a, i], agr.at[a, i])
-            send(src, src, fws.at[a, i], fwr.at[a, i], partner)
+            arrive(src, agr.at[a, i])
+            send(src, src, fws, fwr.at[a], partner)
         acc = up_half(a, core)
-        for i in range(len(CHIPS)):
-            arrive(nall.at[a, other, back(CHIPS[i])], fws.at[a, i], fwr.at[a, i])
-        arrive(nall.at[a, other, chip], fws.at[a, 7], fwr.at[a, 7])
+        arrive(nall.at[a, other], fwr.at[a])
         acc = acc + up_half(a, other)
         hid = (acc * (0.5 * (1.0 + erf(acc * (0.5**0.5))))).astype(BF16)
         for g in (0, 4):
             for i in range(g, g + 4):
                 pre2_s[a, i] = unit_term(hid, a, order[i], other).astype(BF16)
             for i in range(g, g + 4):
-                send(pre2_s.at[a, i], pre2_r.at[a, i], p2s.at[a, i], p2r.at[a, i], partner)
+                send(pre2_s.at[a, i], pre2_r.at[a, i], p2s, p2r.at[a, g // 4], partner)
         for i, off in enumerate(order):
             outk[i] = unit_term(hid, a, off, core)
         for i, off in enumerate(order):
-            arrive(pre2_r.at[a, i], p2s.at[a, i], p2r.at[a, i])
+            if i % 4 == 0:
+                arrive(pre2_r.at[a, pl.ds(i, 4)], p2r.at[a, i // 4])
             t = outk[i] + pre2_r[a, i].astype(F32)
             if i < len(CHIPS):
                 rs2_s[a, i] = t.astype(BF16)
-                send(rs2_s.at[a, i], rs2_r.at[a, i], r2s.at[a, i], r2r.at[a, i], chip_dev(off))
+                send(rs2_s.at[a, i], rs2_r.at[a, i], r2s, r2r.at[a], chip_dev(off))
             else:
                 kept[a] = t
-    flush(len(sends) - len(CHIPS))
+    sent(zsend, pzs)
+    sent(pre_s, p1s)
+    sent(rs_r, r1s)
+    sent(st_s, sts)
+    sent(rs_r, ags)
+    sent(nall.at[0], fws)
+    sent(pre2_s, p2s)
     row_i = lax.broadcasted_iota(jnp.int32, (HR, COLS), 0)
     for a in range(2):
         out = kept[a]
-        for i in reversed(range(len(CHIPS))):
-            arrive(rs2_r.at[a, i], r2s.at[a, i], r2r.at[a, i])
+        arrive(rs2_r.at[a], r2r.at[a])
+        for i in range(len(CHIPS)):
             out = out + rs2_r[a, i].astype(F32)
         lay_out[rows_of(a), :] = jnp.where(row_i + a * HR < my_len, out, 0.0).astype(BF16)
-    for cp in sends:
-        cp.wait_send()
+    sent(rs2_s, r2s)
 
 
 def hand_over(att_ref, lay_ref, att_out, lay_out):
@@ -530,8 +553,8 @@
             vm((NZH, KB, ROWS), F32),
             vm((NZH, 2, DH, ROWS), F32),
             vm((16, ROWS), F32),
-            vm((3, 2, SLOT, ROWS), BF16),
-            vm((3, 2, SLOT, ROWS), BF16),
+            vm((2, 3, SLOT, ROWS), BF16),
+            vm((2, 3, SLOT, ROWS), BF16),
             vm((ROWS, 512), F32),
             vm((n, ROWS, 512), BF16),
             vm((n, ROWS, 512), BF16),
@@ -547,28 +570,31 @@
             vm((2, 8, HR, COLS), BF16),
             vm((2, nc, HR, COLS), BF16),
             vm((2, nc, HR, COLS), BF16),
-            dma((40,)),
-            dma((3,)),
-            dma((3,)),
-            dma((2, 2, 2)),
+            dma((8,)),
+            pltpu.SemaphoreType.REGULAR,
+            pltpu.SemaphoreType.REGULAR,
+            pltpu.SemaphoreType.REGULAR,
+            dma(()),
+            dma(()),
+            dma(()),
+            dma(()),
+            dma((NX - 1, 2, 2)),
+            dma(()),
+            dma((2,)),
+            dma(()),
+            dma((n,)),
+            dma(()),
+            dma((2,)),
+            dma(()),
+            dma((2,)),
+            dma(()),
+            dma((2, nc)),
+            dma(()),
+            dma((2,)),
+            dma(()),
             dma((2, 2)),
-            dma((NX, 2, 2)),
-            dma((3, 2)),
-            dma((3, 2)),
-            dma((n,)),
-            dma((n,)),
-            dma((2, nc)),
-            dma((2, nc)),
+            dma(()),
             dma((2,)),
-            dma((2,)),
-            dma((2, nc)),
-            dma((2, nc)),
-            dma((2, 8)),
-            dma((2, 8)),
-            dma((2, 8)),
-            dma((2, 8)),
-            dma((2, nc)),
-            dma((2, nc)),
         ],
         compiler_params=pltpu.CompilerParams(
             collective_id=0, has_side_effects=True, vmem_limit_bytes=56 * 2**20

time: 68.2 us -> 66 us (0.968)
  Pallas kernels: 67.4 us -> 65.2 us
    pallas_call x1, Pallas kernels: 65.9 us -> 63.7 us  [shards(): pl.pallas_call(kernel, out_shape=[jax.ShapeDtypeStruct((ROWS, COLS), BF16...]
where the time goes in v6:
time: 66 us; the launch traced here: 65.9 us
  Pallas kernels  65.2 us (99%)
    pallas_call x1, Pallas kernels, shards(): pl.pallas_call(kernel, out_shape=[jax.ShapeDtypeStruct((ROWS, COLS), BF16...  63.7 us
    pallas_call x1, Pallas kernels, shards(): pl.pallas_call(hand_over, out_shape=[jax.ShapeDtypeStruct((ROWS, COLS), B...  1.53 us

profile of v6, /device:TPU:1, one launch (start us, length us, event | category | flops | bytes accessed | tf_op | source)
XLA Modules:
  0.0 65.9 jit_solution(10317929341094945255)
XLA Ops:
  0.6 63.7 %prefill_layer.1 = (bf16[128,256]{1,0:T(8,128)(2,1)}, bf16[128,256]{1,0:T(8,128)(2,1)}) custom-call(s32[16]{0:T(128)} %len_ref.1, s32[16]{0:T(128)} %grp_ref.1, s32[16]{0:T(128)} %own_ref.1, bf16[128,256]{1,0:T(8,128)(2,1)} %q_hbm.1, bf16[2,128,256]{2,1,0:T(8,128)(2,1)} %skv_hbm.1, bf16[2,512,256]{2,1,0:T(8,128)(2,1)} %pkv_hbm.1, bf16[128,256]{1,0:T(8,128)(2,1)} %res_hbm.1, ...), custom_call_target="tpu_custom_call" | custom-call | tf_op jit(solution)/shard_map/prefill_layer/pallas_call | solution.py:535
  64.3 1.5 %hand_over.1 = (bf16[128,256]{1,0:T(8,128)(2,1)}, bf16[128,256]{1,0:T(8,128)(2,1)}) custom-call(bf16[128,256]{1,0:T(8,128)(2,1)} %get-tuple-element.4.att_ref, bf16[128,256]{1,0:T(8,128)(2,1)} %get-tuple-element.5.lay_ref), custom_call_target="tpu_custom_call" | custom-call | tf_op jit(solution)/shard_map/hand_over/pallas_call | solution.py:616
